TPU v7x, 128 devices: a whole 4x4x4 slice. The times are simulated.
128 devices in a mesh: gx: 32 (over z, y, core), gy: 4 (over x).
Axes of the slice: x: 4, y: 4, z: 4, core: 2. Of those that a mesh axis runs over, the one named last changes fastest.
Arguments:
- initial_state: float32 [32, 2, 256, 4096], P(None, None, 'gy', 'gx'), may hold values from -34 to 34
- velocity: float32 [3, 2, 256, 4096], P(None, None, 'gy', 'gx'), may hold values from -0.3 to 0.3
- diffusivity: float32 [32], replicated, may hold values from 0.02 to 0.15
- reaction_rate: float32 [32], replicated, may hold values from 0.05 to 0.5
- start_basis: bfloat16 [4096, 128], replicated, may hold values from -0.09375 to 0.09375
Outputs:
- evolved: float32 [32, 2, 256, 4096], P(None, None, 'gy', 'gx')
- factor: bfloat16 [4096, 128], P(('gx', 'gy'))
- subspace_core: float32 [32, 2, 256, 128], P('gx', None, 'gy')
All inputs are finite; a program needn't handle non-finite values.
Results may differ from a plain program's by a relative error of at most 0.012.
Values may be sent and summed in bfloat16 or wider, within the bound.
A program may use at most 64 MiB of HBM per device.

v0:
```python
import jax
import jax.numpy as jnp
from jax import lax
from jax.experimental import pallas as pl
from jax.experimental.pallas import tpu as pltpu
from jax.sharding import PartitionSpec as P

SECTIONS = 4
NS_STEPS = 5
GROUPS = 4
MESH = pl.DeviceIdType.MESH
F32 = jnp.float32
BF16 = jnp.bfloat16


def rolled(x, shift):
    return pltpu.roll(x, shift, 1)


def full_dot(a, b):
    return jnp.dot(a, b, precision=lax.Precision.HIGHEST, preferred_element_type=F32)


def kernel(
    init_hbm, vel_hbm, kappa_ref, rate_ref, basis_hbm,
    evolved_hbm, factor_ref, core_ref,
    state, vel, basis, edge_acc, x_send, x_left, x_right, y_send, y_recv,
    own_cols, own_t, cols, proj, image_part, image_all, image_own, mixing,
    load_sem, out_sem, xs_sem, xr_sem, ys_sem, yr_sem, as_sem, ar_sem, gs_sem, gr_sem, is_sem, ir_sem,
):
    species = state.shape[1]
    ny = state.shape[3] - 16
    per = species // GROUPS
    ngx, ngy = lax.axis_size("gx"), lax.axis_size("gy")
    gx, gy = lax.axis_index("gx"), lax.axis_index("gy")
    right, left = lax.rem(gx + 1, ngx), lax.rem(gx + ngx - 1, ngx)
    north, south = lax.rem(gy + 1, ngy), lax.rem(gy + ngy - 1, ngy)
    lane = lax.broadcasted_iota(jnp.int32, (ny, 128), 1)

    def load_state(g):
        return pltpu.make_async_copy(
            init_hbm.at[pl.ds(g * per, per)],
            state.at[0, pl.ds(g * per, per), :, pl.ds(8, ny), :],
            load_sem.at[g],
        )

    load_vel = pltpu.make_async_copy(vel_hbm, vel, load_sem.at[GROUPS])
    load_basis = pltpu.make_async_copy(basis_hbm, basis, load_sem.at[GROUPS + 1])
    for g in range(GROUPS):
        load_state(g).start()
    load_vel.start()
    load_basis.start()

    barrier = pltpu.get_barrier_semaphore()

    @pl.loop(1, ngx)
    def _(d):
        pl.semaphore_signal(barrier, 1, device_id={"gx": lax.rem(gx + d, ngx)}, device_id_type=MESH)

    @pl.loop(1, ngy)
    def _(d):
        pl.semaphore_signal(barrier, 1, device_id={"gy": lax.rem(gy + d, ngy)}, device_id_type=MESH)

    def x_copy(e, to_left):
        return pltpu.make_async_remote_copy(
            src_ref=x_send.at[e],
            dst_ref=(x_right if to_left else x_left).at[e],
            send_sem=xs_sem.at[int(to_left)],
            recv_sem=xr_sem.at[int(to_left), e],
            device_id={"gx": left if to_left else right},
            device_id_type=MESH,
        )

    def y_copy(e, to_south):
        d = int(to_south)
        return pltpu.make_async_remote_copy(
            src_ref=y_send.at[d, e],
            dst_ref=y_recv.at[d, e],
            send_sem=ys_sem.at[d],
            recv_sem=yr_sem.at[d, e],
            device_id={"gy": south if to_south else north},
            device_id_type=MESH,
        )

    def pack(e, j, z, new):
        mask = (lane == 2 * j) | (lane == 2 * j + 1)
        rows = pl.ds(z * ny, ny)
        edge_acc[rows, :] = jnp.where(mask, rolled(new, 2 * j + 1), edge_acc[rows, :])
        y_send[0, e, pl.ds(2 * j + z, 1), :] = new[ny - 1 :, :]
        y_send[1, e, pl.ds(2 * j + z, 1), :] = new[:1, :]

    def send_edges(e):
        x_send[e] = edge_acc[...].astype(x_send.dtype)
        x_copy(e, True).start()
        x_copy(e, False).start()
        y_copy(e, True).start()
        y_copy(e, False).start()

    def column_copy(s):
        return pltpu.make_async_remote_copy(
            src_ref=own_cols.at[s],
            dst_ref=cols.at[gx],
            send_sem=as_sem,
            recv_sem=ar_sem.at[gx],
            device_id={"gx": s},
            device_id_type=MESH,
        )

    edge_acc[...] = jnp.zeros_like(edge_acc)

    for g in range(GROUPS):
        load_state(g).wait()

        @pl.loop(0, per)
        def _(j):
            for z in range(2):
                pack(g, j, z, state[0, g * per + j, z, pl.ds(8, ny), :])

        if g == 0:
            pl.semaphore_wait(barrier, ngx + ngy - 2)
        send_edges(g)

    load_vel.wait()
    vel[...] = vel[...] * 0.5
    vel[2, 1] = -vel[2, 1]

    @pl.loop(0, SECTIONS * GROUPS)
    def _(e):
        k, g = e // GROUPS, lax.rem(e, GROUPS)
        now = lax.rem(k, 2)
        x_copy(e, True).wait_recv()
        x_copy(e, False).wait_recv()
        y_copy(e, True).wait_recv()
        y_copy(e, False).wait_recv()

        wide = lax.broadcasted_iota(jnp.int32, edge_acc.shape, 1)
        edge_acc[...] = jnp.where(
            lax.rem(wide, 2) == 0, x_left[e].astype(F32), x_right[e].astype(F32)
        )

        @pl.loop(0, per)
        def _(j):
            s = g * per + j
            for z in range(2):
                state[now, s, z, pl.ds(7, 1), :] = y_recv[0, e, pl.ds(2 * j + z, 1), :]
                state[now, s, z, pl.ds(8 + ny, 1), :] = y_recv[1, e, pl.ds(2 * j + z, 1), :]
            kappa, rate = kappa_ref[s], rate_ref[s]
            middle = 1.0 - 6.0 * kappa - rate
            for z in range(2):
                c = state[now, s, z, pl.ds(8, ny), :]
                other = state[now, s, 1 - z, pl.ds(8, ny), :]
                up = state[now, s, z, pl.ds(9, ny), :]
                down = state[now, s, z, pl.ds(7, ny), :]
                halo = rolled(edge_acc[pl.ds(z * ny, ny), :], 127 - 2 * j)
                east = rolled(jnp.where(lane == 0, halo, c), 127)
                west = rolled(jnp.where(lane == 127, halo, c), 1)
                d = 1.0 + c * c
                seed = pl.reciprocal(d, approx=True)
                inverse = seed * (2.0 - d * seed)
                new = (
                    c * (middle + rate * inverse)
                    + kappa * ((east + west) + (up + down))
                    + (kappa - vel[2, z]) * other
                    - vel[0, z] * (east - west)
                    - vel[1, z] * (up - down)
                )
                state[1 - now, s, z, pl.ds(8, ny), :] = new

        @pl.when(k < SECTIONS - 1)
        def _():
            @pl.loop(0, per)
            def _(j):
                for z in range(2):
                    pack(e + GROUPS, j, z, state[1 - now, g * per + j, z, pl.ds(8, ny), :])

            send_edges(e + GROUPS)

        @pl.when(k == SECTIONS - 1)
        def _():
            @pl.loop(0, per)
            def _(j):
                s = g * per + j
                for z in range(2):
                    own_cols[s, pl.ds(z * ny, ny), :] = state[0, s, z, pl.ds(8, ny), :].astype(BF16)

            @pl.loop(0, per)
            def _(j):
                s = g * per + lax.rem(j + gx, per)

                @pl.when(s != gx)
                def _():
                    column_copy(s).start()

            pltpu.make_async_copy(
                state.at[0, pl.ds(g * per, per), :, pl.ds(8, ny), :],
                evolved_hbm.at[pl.ds(g * per, per)],
                out_sem,
            ).start()

    def column_arrival(j):
        return pltpu.make_async_copy(cols.at[j], cols.at[j], ar_sem.at[j])

    cols[gx] = own_cols[gx]

    @pl.loop(0, species)
    def _(s):
        own_t[s] = own_cols[s].T

    load_basis.wait()

    def project_step(j):
        rows = pl.ds(pl.multiple_of(j * 128, 128), 128)
        return jnp.dot(cols[j], basis[rows, :], preferred_element_type=F32)

    def project_next(d, total):
        j = lax.rem(gx + ngx - d, ngx)
        column_arrival(j).wait()
        return total + project_step(j)

    project = lax.fori_loop(1, ngx, project_next, project_step(gx))
    proj[gx] = project.astype(BF16)

    core = lax.rem(gx, 2)
    stride_a = 2 + 6 * core
    stride_b = 8 - 6 * core
    pos_a = lax.rem(gx // stride_a, 4)
    pos_b = lax.rem(gx // stride_b, 4)
    sibling = gx + 1 - 2 * core

    def slot_of(a, b):
        return lax.rem(a, 4) * stride_a + lax.rem(b, 4) * stride_b + core

    def gather(held, which, use):
        def send(slot, peer):
            pltpu.make_async_remote_copy(
                src_ref=held.at[slot],
                dst_ref=held.at[slot],
                send_sem=gs_sem.at[which],
                recv_sem=gr_sem.at[which, slot],
                device_id={"gx": peer},
                device_id_type=MESH,
            ).start()

        def arrival(slot):
            pltpu.make_async_copy(held.at[slot], held.at[slot], gr_sem.at[which, slot]).wait()

        order = (1, 3, 2)
        for d in order:
            send(gx, slot_of(pos_a + d, pos_b))
        for d in order:
            send(gx, slot_of(pos_a, pos_b + d))
        send(gx, sibling)
        total = use(gx)
        for d in order:
            slot = slot_of(pos_a + d, pos_b)
            arrival(slot)
            for f in order:
                send(slot, slot_of(pos_a, pos_b + f))
            send(slot, sibling)
            total += use(slot)
        for d in (0, 1, 3, 2):
            for f in order:
                slot = slot_of(pos_a + d, pos_b + f)
                arrival(slot)
                send(slot, sibling)
                total += use(slot)

        def other(i, total):
            slot = 2 * i + 1 - core
            arrival(slot)
            return total + use(slot)

        return lax.fori_loop(0, ngx // 2, other, total)

    def gather_done(held, which):
        for size in (16, 15):
            part = held.at[pl.ds(0, size)]
            pltpu.make_async_copy(part, part, gs_sem.at[which]).wait()

    part = gather(proj, 0, lambda s: jnp.dot(own_t[s], proj[s], preferred_element_type=F32))

    image_part[gy] = part.astype(BF16)

    def image_copy(d):
        return pltpu.make_async_remote_copy(
            src_ref=image_part.at[gy],
            dst_ref=image_part.at[gy],
            send_sem=is_sem.at[d],
            recv_sem=ir_sem.at[gy],
            device_id={"gy": lax.rem(gy + d, ngy)},
            device_id_type=MESH,
        )

    for d in (1, 3, 2):
        image_copy(d).start()
    for d in (1, 3, 2):
        slot = lax.rem(gy + d, ngy)
        pltpu.make_async_copy(image_part.at[slot], image_part.at[slot], ir_sem.at[slot]).wait()
    image_own[...] = (image_part[0].astype(F32) + image_part[1].astype(F32)) + (
        image_part[2].astype(F32) + image_part[3].astype(F32)
    )
    image_all[gx] = image_own[...].astype(BF16)

    contract_rows = (((0,), (0,)), ((), ()))

    def use_image(s):
        block = image_all[s]
        gram = lax.dot_general(block, block, contract_rows, preferred_element_type=F32)
        carried = jnp.dot(cols[s], block, preferred_element_type=F32)
        return jnp.concatenate([gram, carried], axis=0)

    both = gather(image_all, 1, use_image)
    gram, carried = both[:128], both[128:]

    row = lax.broadcasted_iota(jnp.int32, (128, 128), 0)
    column = lax.broadcasted_iota(jnp.int32, (128, 128), 1)
    identity = jnp.where(row == column, 1.0, 0.0).astype(F32)
    count = 128.0 * ngx
    trace = jnp.sum(gram * identity, keepdims=True)
    squared = count / (trace + 1e-6)
    gram = gram * (squared / count)
    mix = jnp.sqrt(squared) * identity
    for step in range(NS_STEPS):
        poly = 1.5 * identity - 0.5 * gram
        mix = full_dot(mix, poly)
        if step < NS_STEPS - 1:
            gram = full_dot(poly, full_dot(gram, poly))
    mixing[...] = mix

    rows = pl.ds(pl.multiple_of(gy * 32, 32), 32)
    factor_ref[...] = full_dot(image_own[rows, :], mix).astype(BF16)
    result = full_dot(carried, mix) * (count ** -0.5)
    core_ref[0, 0] = result[:ny]
    core_ref[0, 1] = result[ny:]

    for d in range(2):
        pltpu.make_async_copy(x_send, x_send, xs_sem.at[d]).wait()
        pltpu.make_async_copy(y_send.at[d], y_send.at[d], ys_sem.at[d]).wait()
    for g in range(GROUPS):
        pltpu.make_async_copy(
            state.at[0, pl.ds(g * per, per), :, pl.ds(8, ny), :],
            evolved_hbm.at[pl.ds(g * per, per)],
            out_sem,
        ).wait()
    sent = own_cols.at[pl.ds(0, ngx - 1)]
    pltpu.make_async_copy(sent, sent, as_sem).wait()
    gather_done(proj, 0)
    gather_done(image_all, 1)
    for d in (1, 3, 2):
        image_copy(d).wait_send()


def shards(initial_state, velocity, diffusivity, reaction_rate, start_basis):
    species, nz, ny, nx = initial_state.shape
    ngx, ngy = lax.axis_size("gx"), lax.axis_size("gy")
    rank = start_basis.shape[1]
    exchanges = SECTIONS * GROUPS
    rows = 2 * species // GROUPS
    anywhere = pl.BlockSpec(memory_space=pl.ANY)
    scalars = pl.BlockSpec(memory_space=pltpu.SMEM)
    vmem = pl.BlockSpec(memory_space=pltpu.VMEM)
    dma = pltpu.SemaphoreType.DMA
    return pl.pallas_call(
        kernel,
        out_shape=(
            jax.ShapeDtypeStruct(initial_state.shape, F32),
            jax.ShapeDtypeStruct((ny // 2, rank), BF16),
            jax.ShapeDtypeStruct((1, nz, ny, rank), F32),
        ),
        in_specs=[anywhere, anywhere, scalars, scalars, anywhere],
        out_specs=(anywhere, vmem, vmem),
        scratch_shapes=[
            pltpu.VMEM((2, species, nz, ny + 16, nx), F32),
            pltpu.VMEM((3, nz, ny, nx), F32),
            pltpu.VMEM(start_basis.shape, BF16),
            pltpu.VMEM((nz * ny, nx), F32),
            pltpu.VMEM((exchanges, nz * ny, nx), BF16),
            pltpu.VMEM((exchanges, nz * ny, nx), BF16),
            pltpu.VMEM((exchanges, nz * ny, nx), BF16),
            pltpu.VMEM((2, exchanges, rows, nx), F32),
            pltpu.VMEM((2, exchanges, rows, nx), F32),
            pltpu.VMEM((species, nz * ny, nx), BF16),
            pltpu.VMEM((species, nx, nz * ny), BF16),
            pltpu.VMEM((species, nz * ny, nx), BF16),
            pltpu.VMEM((ngx, nz * ny, rank), BF16),
            pltpu.VMEM((ngy, nx, rank), BF16),
            pltpu.VMEM((ngx, nx, rank), BF16),
            pltpu.VMEM((nx, rank), F32),
            pltpu.VMEM((rank, rank), F32),
            dma((GROUPS + 2,)),
            dma,
            dma((2,)),
            dma((2, exchanges)),
            dma((2,)),
            dma((2, exchanges)),
            dma,
            dma((ngx,)),
            dma((2,)),
            dma((2, ngx)),
            dma((ngy,)),
            dma((ngy,)),
        ],
        compiler_params=pltpu.CompilerParams(
            collective_id=0, has_side_effects=True, vmem_limit_bytes=48 << 20
        ),
    )(initial_state, velocity, diffusivity, reaction_rate, start_basis)


def solution(mesh):
    return jax.shard_map(
        shards,
        mesh=mesh,
        in_specs=(P(None, None, "gy", "gx"), P(None, None, "gy", "gx"), P(), P(), P()),
        out_specs=(P(None, None, "gy", "gx"), P(("gx", "gy"), None), P("gx", None, "gy", None)),
        check_vma=False,
    )
```

profile of v0, /device:TPU:1, one launch (start us, length us, event | category | flops | bytes accessed | tf_op | source)
XLA Modules:
  0.0 110.7 jit_solution(4337816820654541577)
XLA Ops:
  0.6 0.0 copy-start
  0.6 1.6 %copy-done = f32[32,2,64,128]{3,2,1,0:T(8,128)S(1)} copy-done((f32[32,2,64,128]{3,2,1,0:T(8,128)S(1)}, f32[32,2,64,128]{3,2,1,0:T(8,128)}, u32[]{:S(2)}) %copy-start) | copy-done | bytes 2097176
  2.2 0.0 copy-start.1
  2.2 1.2 %copy-done.1 = bf16[4096,128]{1,0:T(8,128)(2,1)S(1)} copy-done((bf16[4096,128]{1,0:T(8,128)(2,1)S(1)}, bf16[4096,128]{1,0:T(8,128)(2,1)}, u32[]{:S(2)}) %copy-start.1) | copy-done | bytes 1048600
  3.4 0.0 copy-start.2
  3.5 0.9 copy-done.2
  4.4 0.0 copy-start.3
  4.4 0.7 copy-done.3
  5.0 0.0 copy-start.4
  5.0 0.7 copy-done.4
  5.7 102.4 %shard_map.76 = (f32[32,2,64,128]{3,2,1,0:T(8,128)S(1)}, bf16[32,128]{1,0:T(8,128)(2,1)S(1)}, f32[1,2,64,128]{3,2,1,0:T(8,128)S(1)}) custom-call(f32[32,2,64,128]{3,2,1,0:T(8,128)S(1)} %copy-done, f32[3,2,64,128]{3,2,1,0:T(8,128)S(1)} %copy-done.2, f32[32]{0:T(128)S(1)} %copy-done.3, f32[32]{0:T(128)S(1)} %copy-done.4, bf16[4096,128]{1,0:T(8,128)(2,1)S(1)} %copy-done.1), custom_call_target="tpu_custom_call" | custom-call | tf_op jit(solution)/shard_map/pallas_call | solution.py:363
  108.1 1.3 %copy.11 = f32[32,2,64,128]{3,2,1,0:T(8,128)} copy(f32[32,2,64,128]{3,2,1,0:T(8,128)S(1)} %get-tuple-element.6) | data formatting | bytes 4194304
  109.5 0.6 copy.12
  110.1 0.6 copy.13
Async XLA Ops:
  0.6 1.6 %copy-start = (f32[32,2,64,128]{3,2,1,0:T(8,128)S(1)}, f32[32,2,64,128]{3,2,1,0:T(8,128)}, u32[]{:S(2)}) copy-start(f32[32,2,64,128]{3,2,1,0:T(8,128)} %init_hbm.1) | copy-start | bytes 6291460
  2.2 1.2 %copy-start.1 = (bf16[4096,128]{1,0:T(8,128)(2,1)S(1)}, bf16[4096,128]{1,0:T(8,128)(2,1)}, u32[]{:S(2)}) copy-start(bf16[4096,128]{1,0:T(8,128)(2,1)} %basis_hbm.1) | copy-start | bytes 3145732
  3.4 0.9 copy-start.2
  4.4 0.7 copy-start.3
  5.0 0.7 copy-start.4
where the time goes:
time: 111 us
  Pallas kernels  102 us (92%)
  local copies, waits for them, and re-layouts  7.59 us (7%)
    pallas_call x1, Pallas kernels, shards(): pl.pallas_call(kernel, out_shape=(jax.ShapeDtypeStruct(initial_state.shap...  102 us
    unnamed x13, local copies, waits for them, and re-layouts  7.59 us

commit v1 on v0

v1 whole, which is shorter than its diff:
```python
import functools

import jax
import jax.numpy as jnp
from jax import lax
from jax.experimental import pallas as pl
from jax.experimental.pallas import tpu as pltpu
from jax.sharding import PartitionSpec as P

SECTIONS = 4
NS_STEPS = 5
GROUPS = 4
UNROLL = 2
VMEM_LIMIT = 32 << 20
MESH = pl.DeviceIdType.MESH
F32 = jnp.float32
BF16 = jnp.bfloat16


def rolled(x, shift):
    return pltpu.roll(x, shift, 1)


def full_dot(a, b):
    return jnp.dot(a, b, precision=lax.Precision.HIGHEST, preferred_element_type=F32)


def kernel(
    init_hbm, vel_hbm, kappa_hbm, rate_hbm, basis_hbm,
    evolved_ref, gram_ref, carried_ref, image_ref,
    state, state_b, vel, kappa_ref, rate_ref, basis, halos, x_send, x_left, x_right, y_send, y_recv,
    own_cols, own_t, cols, proj, image_part, image_all, image_own,
    load_sem, xs_sem, xr_sem, ys_sem, yr_sem, as_sem, ar_sem, gs_sem, gr_sem, is_sem, ir_sem,
):
    species = state.shape[0]
    ny = state.shape[2] - 16
    per = species // GROUPS
    ngx, ngy = lax.axis_size("gx"), lax.axis_size("gy")
    gx, gy = lax.axis_index("gx"), lax.axis_index("gy")
    right, left = lax.rem(gx + 1, ngx), lax.rem(gx + ngx - 1, ngx)
    north, south = lax.rem(gy + 1, ngy), lax.rem(gy + ngy - 1, ngy)
    core = lax.rem(gx, 2)
    half = ngx // 2
    lane = lax.broadcasted_iota(jnp.int32, (ny, 128), 1)
    pair = lane // 2

    def block(x):
        at = lax.rem(x, 2) * half + x // 2
        return pl.ds(pl.multiple_of(at * 128, 128), 128)

    def load_state(g):
        return pltpu.make_async_copy(
            init_hbm.at[pl.ds(g * per, per)],
            state.at[pl.ds(g * per, per), :, pl.ds(8, ny), :],
            load_sem.at[g],
        )

    load_vel = pltpu.make_async_copy(vel_hbm, vel, load_sem.at[GROUPS])
    load_kappa = pltpu.make_async_copy(kappa_hbm, kappa_ref, load_sem.at[GROUPS + 2])
    load_rate = pltpu.make_async_copy(rate_hbm, rate_ref, load_sem.at[GROUPS + 3])
    for g in range(GROUPS):
        load_state(g).start()
    load_kappa.start()
    load_rate.start()
    load_vel.start()

    barrier = pltpu.get_barrier_semaphore()

    @pl.loop(1, ngx)
    def _(d):
        pl.semaphore_signal(barrier, 1, device_id={"gx": lax.rem(gx + d, ngx)}, device_id_type=MESH)

    @pl.loop(1, ngy)
    def _(d):
        pl.semaphore_signal(barrier, 1, device_id={"gy": lax.rem(gy + d, ngy)}, device_id_type=MESH)

    def x_copy(e, to_left):
        return pltpu.make_async_remote_copy(
            src_ref=x_send.at[e],
            dst_ref=(x_right if to_left else x_left).at[e],
            send_sem=xs_sem.at[int(to_left)],
            recv_sem=xr_sem.at[int(to_left), e],
            device_id={"gx": left if to_left else right},
            device_id_type=MESH,
        )

    def y_copy(e, to_south):
        d = int(to_south)
        return pltpu.make_async_remote_copy(
            src_ref=y_send.at[d, e],
            dst_ref=y_recv.at[d, e],
            send_sem=ys_sem.at[d],
            recv_sem=yr_sem.at[d, e],
            device_id={"gy": south if to_south else north},
            device_id_type=MESH,
        )

    def column_copy(s):
        return pltpu.make_async_remote_copy(
            src_ref=own_cols.at[s],
            dst_ref=cols.at[:, block(gx)],
            send_sem=as_sem,
            recv_sem=ar_sem.at[gx],
            device_id={"gx": s},
            device_id_type=MESH,
        )

    def send_edges(e, now, first):
        for z in range(2):
            packed = jnp.zeros((ny, 128), F32)
            for j in range(per):
                cells = now[first + j, z, pl.ds(8, ny), :]
                packed = jnp.where(pair == j, rolled(cells, 2 * j + 1), packed)
                y_send[0, e, pl.ds(2 * j + z, 1), :] = now[first + j, z, pl.ds(7 + ny, 1), :]
                y_send[1, e, pl.ds(2 * j + z, 1), :] = now[first + j, z, pl.ds(8, 1), :]
            x_send[e, pl.ds(z * ny, ny), :] = packed.astype(x_send.dtype)
        x_copy(e, True).start()
        x_copy(e, False).start()
        y_copy(e, True).start()
        y_copy(e, False).start()

    load_state(0).wait()
    pl.semaphore_wait(barrier, ngx + ngy - 2)
    send_edges(0, state, 0)
    for g in range(1, GROUPS):
        load_state(g).wait()

    @pl.loop(1, GROUPS)
    def _(g):
        send_edges(g, state, g * per)

    @pl.loop(0, ngx)
    def _(x):
        pltpu.make_async_copy(
            basis_hbm.at[pl.ds(pl.multiple_of(x * 128, 128), 128)], basis.at[block(x)],
            load_sem.at[GROUPS + 1],
        ).start()

    load_vel.wait()
    vel[...] = vel[...] * 0.5
    vel[2, 1] = -vel[2, 1]
    load_kappa.wait()
    load_rate.wait()

    def advance(k, g, now, new):
        e = k * GROUPS + g
        last = k == SECTIONS - 1
        x_copy(e, True).wait_recv()
        x_copy(e, False).wait_recv()
        y_copy(e, True).wait_recv()
        y_copy(e, False).wait_recv()

        wide = lax.broadcasted_iota(jnp.int32, halos.shape, 1)
        halos[...] = jnp.where(
            lax.rem(wide, 2) == 0,
            rolled(x_right[e].astype(F32), 127),
            rolled(x_left[e].astype(F32), 1),
        )

        for j in range(per):
            for z in range(2):
                now[g * per + j, z, pl.ds(7, 1), :] = y_recv[0, e, pl.ds(2 * j + z, 1), :]
                now[g * per + j, z, pl.ds(8 + ny, 1), :] = y_recv[1, e, pl.ds(2 * j + z, 1), :]

        @pl.loop(0, per, step=UNROLL)
        def _(j0):
            for i in range(UNROLL):
                j = j0 + i
                s = g * per + j
                kappa, rate = kappa_ref[s], rate_ref[s]
                middle = 1.0 - 6.0 * kappa - rate
                for z in range(2):
                    c = now[s, z, pl.ds(8, ny), :]
                    other = now[s, 1 - z, pl.ds(8, ny), :]
                    up = now[s, z, pl.ds(9, ny), :]
                    down = now[s, z, pl.ds(7, ny), :]
                    halo = rolled(halos[pl.ds(z * ny, ny), :], 127 - 2 * j)
                    east = jnp.where(lane == 127, halo, rolled(c, 127))
                    west = jnp.where(lane == 0, halo, rolled(c, 1))
                    result = (
                        c * (middle + rate * (1.0 / (1.0 + c * c)))
                        + kappa * ((east + west) + (up + down))
                        + (kappa - vel[2, z]) * other
                        - vel[0, z] * (east - west)
                        - vel[1, z] * (up - down)
                    )
                    if last:
                        evolved_ref[s, z] = result
                        own_cols[s, pl.ds(z * ny, ny), :] = result.astype(BF16)
                    else:
                        new[s, z, pl.ds(8, ny), :] = result

        if not last:
            send_edges(e + GROUPS, new, g * per)

    buffers = (state, state_b)
    for k in range(SECTIONS - 1):

        @pl.loop(0, GROUPS)
        def _(g):
            advance(k, g, buffers[k % 2], buffers[(k + 1) % 2])

    @pl.loop(0, GROUPS)
    def _(g):
        advance(SECTIONS - 1, g, buffers[(SECTIONS - 1) % 2], None)

        @pl.loop(0, per)
        def _(j):
            s = g * per + lax.rem(j + gx, per)

            @pl.when(s != gx)
            def _():
                column_copy(s).start()

    def column_arrival(x):
        return pltpu.make_async_copy(cols.at[:, block(x)], cols.at[:, block(x)], ar_sem.at[x])

    cols[:, block(gx)] = own_cols[gx]

    @pl.loop(0, species, step=4)
    def _(s):
        for i in range(4):
            own_t[:, block(s + i)] = own_cols[s + i].T

    basis_all = pltpu.make_async_copy(basis_hbm, basis, load_sem.at[GROUPS + 1])
    basis_all.wait()

    @pl.loop(1, ngx)
    def _(d):
        column_arrival(lax.rem(gx + ngx - d, ngx)).wait()

    proj[block(gx), :] = jnp.dot(cols[...], basis[...], preferred_element_type=F32).astype(BF16)

    stride_a = 2 + 6 * core
    stride_b = 8 - 6 * core
    pos_a = lax.rem(gx // stride_a, 4)
    pos_b = lax.rem(gx // stride_b, 4)
    sibling = gx + 1 - 2 * core

    def device_at(a, b):
        return lax.rem(a, 4) * stride_a + lax.rem(b, 4) * stride_b + core

    def gather(held, which, use):
        def send(x, peer):
            pltpu.make_async_remote_copy(
                src_ref=held.at[block(x)],
                dst_ref=held.at[block(x)],
                send_sem=gs_sem.at[which],
                recv_sem=gr_sem.at[which, x],
                device_id={"gx": peer},
                device_id_type=MESH,
            ).start()

        def arrival(x):
            pltpu.make_async_copy(held.at[block(x)], held.at[block(x)], gr_sem.at[which, x]).wait()

        order = (1, 3, 2)
        for d in order:
            send(gx, device_at(pos_a + d, pos_b))
        for d in order:
            send(gx, device_at(pos_a, pos_b + d))
        send(gx, sibling)
        for d in order:
            x = device_at(pos_a + d, pos_b)
            arrival(x)
            for f in order:
                send(x, device_at(pos_a, pos_b + f))
            send(x, sibling)
        for d in (0, 1, 3, 2):
            for f in order:
                x = device_at(pos_a + d, pos_b + f)
                arrival(x)
                send(x, sibling)
        first = use(core)

        @pl.loop(0, half)
        def _(i):
            arrival(2 * i + 1 - core)

        second = use(1 - core)
        return jax.tree.map(jnp.add, first, second)

    def gather_done(held, which):
        part = held.at[pl.ds(0, (ngx - 1) * 128)]
        pltpu.make_async_copy(part, part, gs_sem.at[which]).wait()

    def span(c):
        return pl.ds(pl.multiple_of(c * (half * 128), half * 128), half * 128)

    part = gather(
        proj, 0, lambda c: jnp.dot(own_t[:, span(c)], proj[span(c), :], preferred_element_type=F32)
    )

    image_part[gy] = part.astype(BF16)

    def image_copy(d):
        return pltpu.make_async_remote_copy(
            src_ref=image_part.at[gy],
            dst_ref=image_part.at[gy],
            send_sem=is_sem.at[d],
            recv_sem=ir_sem.at[gy],
            device_id={"gy": lax.rem(gy + d, ngy)},
            device_id_type=MESH,
        )

    for d in (1, 3, 2):
        image_copy(d).start()
    for d in (1, 3, 2):
        slot = lax.rem(gy + d, ngy)
        pltpu.make_async_copy(image_part.at[slot], image_part.at[slot], ir_sem.at[slot]).wait()
    image_own[...] = (image_part[0].astype(F32) + image_part[1].astype(F32)) + (
        image_part[2].astype(F32) + image_part[3].astype(F32)
    )
    image_all[block(gx), :] = image_own[...].astype(BF16)

    contract_rows = (((0,), (0,)), ((), ()))

    def use_image(c):
        x = image_all[span(c), :]
        return (
            lax.dot_general(x, x, contract_rows, preferred_element_type=F32),
            jnp.dot(cols[:, span(c)], x, preferred_element_type=F32),
        )

    gram, carried = gather(image_all, 1, use_image)

    gram_ref[...] = gram
    carried_ref[...] = carried
    rows = pl.ds(pl.multiple_of(gy * 32, 32), 32)
    image_ref[...] = image_own[rows, :]

    for d in range(2):
        pltpu.make_async_copy(x_send, x_send, xs_sem.at[d]).wait()
        pltpu.make_async_copy(y_send.at[d], y_send.at[d], ys_sem.at[d]).wait()
    sent = own_cols.at[pl.ds(0, ngx - 1)]
    pltpu.make_async_copy(sent, sent, as_sem).wait()
    gather_done(proj, 0)
    gather_done(image_all, 1)
    for d in (1, 3, 2):
        image_copy(d).wait_send()


def finish(count, evolved_ref, gram_ref, carried_ref, image_ref, out_hbm, factor_ref, core_ref, sem):
    writing = pltpu.make_async_copy(evolved_ref, out_hbm, sem)
    writing.start()
    row = lax.broadcasted_iota(jnp.int32, (128, 128), 0)
    column = lax.broadcasted_iota(jnp.int32, (128, 128), 1)
    identity = jnp.where(row == column, 1.0, 0.0).astype(F32)
    gram = gram_ref[...]
    trace = jnp.sum(gram * identity, keepdims=True)
    squared = count / (trace + 1e-6)
    gram = gram * (squared / count)
    mix = jnp.sqrt(squared) * identity
    for step in range(NS_STEPS):
        poly = 1.5 * identity - 0.5 * gram
        mix = full_dot(mix, poly)
        if step < NS_STEPS - 1:
            gram = full_dot(poly, full_dot(gram, poly))

    factor_ref[...] = full_dot(image_ref[...], mix).astype(BF16)
    result = full_dot(carried_ref[...], mix) * (count ** -0.5)
    ny = core_ref.shape[2]
    core_ref[0, 0] = result[:ny]
    core_ref[0, 1] = result[ny:]
    writing.wait()


def shards(initial_state, velocity, diffusivity, reaction_rate, start_basis):
    species, nz, ny, nx = initial_state.shape
    ngx, ngy = lax.axis_size("gx"), lax.axis_size("gy")
    rank = start_basis.shape[1]
    operands = (initial_state, velocity, diffusivity, reaction_rate, start_basis)
    exchanges = SECTIONS * GROUPS
    rows = 2 * species // GROUPS
    hbm = pl.BlockSpec(memory_space=pltpu.HBM)
    vmem = pl.BlockSpec(memory_space=pltpu.VMEM)
    dma = pltpu.SemaphoreType.DMA
    evolved, gram, carried, image = pl.pallas_call(
        kernel,
        out_shape=(
            jax.ShapeDtypeStruct(initial_state.shape, F32),
            jax.ShapeDtypeStruct((rank, rank), F32),
            jax.ShapeDtypeStruct((nz * ny, rank), F32),
            jax.ShapeDtypeStruct((nx // ngy, rank), F32),
        ),
        in_specs=[hbm] * 5,
        out_specs=(vmem,) * 4,
        scratch_shapes=[
            pltpu.VMEM((species, nz, ny + 16, nx), F32),
            pltpu.VMEM((species, nz, ny + 16, nx), F32),
            pltpu.VMEM((3, nz, ny, nx), F32),
            pltpu.SMEM((species,), F32),
            pltpu.SMEM((species,), F32),
            pltpu.VMEM(start_basis.shape, BF16),
            pltpu.VMEM((nz * ny, nx), F32),
            pltpu.VMEM((exchanges, nz * ny, nx), BF16),
            pltpu.VMEM((exchanges, nz * ny, nx), BF16),
            pltpu.VMEM((exchanges, nz * ny, nx), BF16),
            pltpu.VMEM((2, exchanges, rows, nx), F32),
            pltpu.VMEM((2, exchanges, rows, nx), F32),
            pltpu.VMEM((species, nz * ny, nx), BF16),
            pltpu.VMEM((nx, species * nz * ny), BF16),
            pltpu.VMEM((nz * ny, ngx * nx), BF16),
            pltpu.VMEM((species * nz * ny, rank), BF16),
            pltpu.VMEM((ngy, nx, rank), BF16),
            pltpu.VMEM((ngx * nx, rank), BF16),
            pltpu.VMEM((nx, rank), F32),
            dma((GROUPS + 4,)),
            dma((2,)),
            dma((2, exchanges)),
            dma((2,)),
            dma((2, exchanges)),
            dma,
            dma((ngx,)),
            dma((2,)),
            dma((2, ngx)),
            dma((ngy,)),
            dma((ngy,)),
        ],
        compiler_params=pltpu.CompilerParams(
            collective_id=0, has_side_effects=True, vmem_limit_bytes=VMEM_LIMIT
        ),
    )(*(pltpu.with_memory_space_constraint(x, pltpu.HBM) for x in operands))
    return pl.pallas_call(
        functools.partial(finish, float(nx * ngx)),
        out_shape=(
            jax.ShapeDtypeStruct(initial_state.shape, F32),
            jax.ShapeDtypeStruct((nx // ngy, rank), BF16),
            jax.ShapeDtypeStruct((1, nz, ny, rank), F32),
        ),
        in_specs=[pl.BlockSpec(memory_space=pl.ANY), vmem, vmem, vmem],
        out_specs=(hbm, vmem, vmem),
        scratch_shapes=[dma],
        compiler_params=pltpu.CompilerParams(vmem_limit_bytes=8 << 20),
    )(evolved, gram, carried, image)


def solution(mesh):
    return jax.shard_map(
        shards,
        mesh=mesh,
        in_specs=(P(None, None, "gy", "gx"), P(None, None, "gy", "gx"), P(), P(), P()),
        out_specs=(P(None, None, "gy", "gx"), P(("gx", "gy"), None), P("gx", None, "gy", None)),
        check_vma=False,
    )
```

time: 111 us -> 76.9 us (0.69)
  Pallas kernels: 102 us -> 76.1 us
  local copies, waits for them, and re-layouts: 7.59 us -> 0 us
    pallas_call x1, Pallas kernels: 102 us -> 72.9 us  [shards(): pl.pallas_call(kernel, out_shape=(jax.ShapeDtypeStruct(initial_state.shap...]
    unnamed x13 -> x0, local copies, waits for them, and re-layouts: 7.59 us -> none
    pallas_call x0 -> x1, Pallas kernels: none -> 3.17 us  [shards(): pl.pallas_call(functools.partial(finish, float(nx * ngx)), out_shape=(jax...]
where the time goes in v1:
time: 76.9 us; the launch traced here: 76.7 us
  Pallas kernels  76.1 us (99%)
    pallas_call x1, Pallas kernels, shards(): pl.pallas_call(kernel, out_shape=(jax.ShapeDtypeStruct(initial_state.shap...  72.9 us
    pallas_call x1, Pallas kernels, shards(): pl.pallas_call(functools.partial(finish, float(nx * ngx)), out_shape=(jax...  3.17 us

profile of v1, /device:TPU:1, one launch (start us, length us, event | category | flops | bytes accessed | tf_op | source)
XLA Modules:
  0.0 76.7 jit_solution(8400127457596441396)
XLA Ops:
  0.6 72.9 %shard_map.76 = (f32[32,2,64,128]{3,2,1,0:T(8,128)S(1)}, f32[128,128]{1,0:T(8,128)S(1)}, f32[128,128]{1,0:T(8,128)S(1)}, f32[32,128]{1,0:T(8,128)S(1)}) custom-call(f32[32,2,64,128]{3,2,1,0:T(8,128)} %init_hbm.1, f32[3,2,64,128]{3,2,1,0:T(8,128)} %vel_hbm.1, f32[32]{0:T(128)} %kappa_hbm.1, f32[32]{0:T(128)} %rate_hbm.1, bf16[4096,128]{1,0:T(8,128)(2,1)} %basis_hbm.1), custom_call_target="tpu_custom_call" | custom-call | tf_op jit(solution)/shard_map/pallas_call | solution.py:378
  73.6 3.2 %shard_map.77 = (f32[32,2,64,128]{3,2,1,0:T(8,128)}, bf16[32,128]{1,0:T(8,128)(2,1)}, f32[1,2,64,128]{3,2,1,0:T(8,128)}) custom-call(f32[32,2,64,128]{3,2,1,0:T(8,128)S(1)} %get-tuple-element.7.evolved_ref, f32[128,128]{1,0:T(8,128)S(1)} %get-tuple-element.8.gram_ref, f32[128,128]{1,0:T(8,128)S(1)} %get-tuple-element.9.carried_ref, ...), custom_call_target="tpu_custom_call" | custom-call | tf_op jit(solution)/shard_map/pallas_call | solution.py:424

commit v2 on v1

v2 whole, which is shorter than its diff:
```python
import functools

import jax
import jax.numpy as jnp
from jax import lax
from jax.experimental import pallas as pl
from jax.experimental.pallas import tpu as pltpu
from jax.sharding import PartitionSpec as P

SECTIONS = 4
NS_STEPS = 5
GROUPS = 4
UNROLL = 2
VMEM_LIMIT = 32 << 20
MESH = pl.DeviceIdType.MESH
F32 = jnp.float32
BF16 = jnp.bfloat16


def rolled(x, shift):
    return pltpu.roll(x, shift, 1)


def halves(x):
    high = x.astype(BF16)
    return high, (x - high.astype(F32)).astype(BF16)


def full_dot(a, b):
    a_high, a_low = halves(a)
    b_high, b_low = halves(b)
    return jnp.dot(
        jnp.concatenate([a_high, a_high, a_low], axis=1),
        jnp.concatenate([b_high, b_low, b_high], axis=0),
        preferred_element_type=F32,
    )


def tree_sum(terms):
    while len(terms) > 1:
        terms = [a + b for a, b in zip(terms[::2], terms[1::2])]
    return terms[0]


def mixing(gram, count):
    row = lax.broadcasted_iota(jnp.int32, gram.shape, 0)
    column = lax.broadcasted_iota(jnp.int32, gram.shape, 1)
    identity = jnp.where(row == column, 1.0, 0.0).astype(F32)
    trace = jnp.sum(gram * identity, keepdims=True)
    squared = count / (trace + 1e-6)
    gram = gram * (squared / count)
    mix = jnp.sqrt(squared) * identity
    for step in range(NS_STEPS):
        poly = 1.5 * identity - 0.5 * gram
        mix = full_dot(mix, poly)
        if step < NS_STEPS - 1:
            gram = full_dot(poly, full_dot(gram, poly))
    return mix


def kernel(
    init_hbm, vel_hbm, kappa_hbm, rate_hbm, basis_hbm,
    evolved_ref, mix_ref, carried_ref, image_ref,
    state, state_b, vel, kappa_ref, rate_ref, basis, halos, x_send, x_left, x_right, y_send, y_recv,
    pairs, outbox, own_t, part_box, part_sum, carry_box, carry_sum, proj, image_part, image_pair, image_own, gram_part, gram_sum, gram_all,
    load_sem, xs_sem, xr_sem, ys_sem, yr_sem, cs_sem, cr_sem, as_sem, ar_sem, gs_sem, gr_sem, is_sem, ir_sem, ps_sem, pr_sem, ms_sem, mr_sem, ts_sem, tr_sem,
):
    species = state.shape[0]
    ny = state.shape[2] - 16
    per = species // GROUPS
    ngx, ngy = lax.axis_size("gx"), lax.axis_size("gy")
    gx, gy = lax.axis_index("gx"), lax.axis_index("gy")
    right, left = lax.rem(gx + 1, ngx), lax.rem(gx + ngx - 1, ngx)
    north, south = lax.rem(gy + 1, ngy), lax.rem(gy + ngy - 1, ngy)
    core = lax.rem(gx, 2)
    half = ngx // 2
    chip = gx // 2
    sibling = gx + 1 - 2 * core
    own_lanes = pl.ds(pl.multiple_of(core * 128, 128), 128)
    own_slot = core * half
    pairs_per = per // 2
    lane = lax.broadcasted_iota(jnp.int32, (ny, 128), 1)
    pair = lane // 2

    def block(x):
        at = lax.rem(x, 2) * half + x // 2
        return pl.ds(pl.multiple_of(at * 128, 128), 128)

    def load_state(g):
        return pltpu.make_async_copy(
            init_hbm.at[pl.ds(g * per, per)],
            state.at[pl.ds(g * per, per), :, pl.ds(8, ny), :],
            load_sem.at[g],
        )

    load_vel = pltpu.make_async_copy(vel_hbm, vel, load_sem.at[GROUPS])
    load_kappa = pltpu.make_async_copy(kappa_hbm, kappa_ref, load_sem.at[GROUPS + 2])
    load_rate = pltpu.make_async_copy(rate_hbm, rate_ref, load_sem.at[GROUPS + 3])
    for g in range(GROUPS):
        load_state(g).start()
    load_kappa.start()
    load_rate.start()
    load_vel.start()

    barrier = pltpu.get_barrier_semaphore()

    @pl.loop(1, half)
    def _(d):
        peer = lax.rem(gx + 2 * d, ngx)
        pl.semaphore_signal(barrier, 1, device_id={"gx": peer}, device_id_type=MESH)

    for peer in (left, right):
        pl.semaphore_signal(barrier, 1, device_id={"gx": peer}, device_id_type=MESH)

    @pl.loop(1, ngy)
    def _(d):
        peer = lax.rem(gy + d, ngy)
        pl.semaphore_signal(barrier, 1, device_id={"gy": peer}, device_id_type=MESH)
        pl.semaphore_signal(barrier, 1, device_id={"gx": sibling, "gy": peer}, device_id_type=MESH)

    def x_copy(e, to_left):
        return pltpu.make_async_remote_copy(
            src_ref=x_send.at[e],
            dst_ref=(x_right if to_left else x_left).at[e],
            send_sem=xs_sem.at[int(to_left)],
            recv_sem=xr_sem.at[int(to_left), e],
            device_id={"gx": left if to_left else right},
            device_id_type=MESH,
        )

    def y_copy(e, to_south):
        d = int(to_south)
        return pltpu.make_async_remote_copy(
            src_ref=y_send.at[d, e],
            dst_ref=y_recv.at[d, e],
            send_sem=ys_sem.at[d],
            recv_sem=yr_sem.at[d, e],
            device_id={"gy": south if to_south else north},
            device_id_type=MESH,
        )

    def pair_copy(g):
        return pltpu.make_async_remote_copy(
            src_ref=outbox.at[pl.ds(g * pairs_per, pairs_per)],
            dst_ref=pairs.at[pl.ds(g * pairs_per, pairs_per), :, own_lanes],
            send_sem=cs_sem,
            recv_sem=cr_sem.at[g],
            device_id={"gx": sibling},
            device_id_type=MESH,
        )

    def part_copy(box, total, which, i):
        return pltpu.make_async_remote_copy(
            src_ref=box.at[i],
            dst_ref=total.at[chip],
            send_sem=as_sem.at[which],
            recv_sem=ar_sem.at[which, chip],
            device_id={"gx": 2 * i + core},
            device_id_type=MESH,
        )

    def send_parts(box, total, which, first, count, rows):
        cells = pairs[pl.ds(first, count)].reshape(count * pairs.shape[1], pairs.shape[2])
        parts = jnp.dot(cells, rows, preferred_element_type=F32).astype(BF16)
        box[pl.ds(first, count)] = parts.reshape(count, *box.shape[1:])

        @pl.loop(first, first + count)
        def _(i):
            @pl.when(i != chip)
            def _():
                part_copy(box, total, which, i).start()

    def summed(box, total, which):
        @pl.loop(1, half)
        def _(d):
            slot = lax.rem(chip + half - d, half)
            pltpu.make_async_copy(total.at[slot], total.at[slot], ar_sem.at[which, slot]).wait()

        total[chip] = box[chip]
        return tree_sum([total[i].astype(F32) for i in range(half)])

    def pack_edges(e, now, first):
        packed = jnp.zeros((ny, 128), F32)
        for f in range(2 * per):
            field = now.at[first + f // 2, f % 2]
            packed = jnp.where(pair == f, rolled(field[pl.ds(8, ny), :], 2 * f + 1), packed)
            y_send[0, e, pl.ds(f, 1), :] = field[pl.ds(7 + ny, 1), :]
            y_send[1, e, pl.ds(f, 1), :] = field[pl.ds(8, 1), :]
        x_send[e] = packed.astype(x_send.dtype)

    def send_edges(e):
        x_copy(e, True).start()
        x_copy(e, False).start()
        y_copy(e, True).start()
        y_copy(e, False).start()

    for g in range(GROUPS):
        load_state(g).wait()

    @pl.loop(0, GROUPS)
    def _(g):
        pack_edges(g, state, g * per)

    pl.semaphore_wait(barrier, half + 2 * ngy - 1)

    @pl.loop(0, GROUPS)
    def _(g):
        send_edges(g)

    basis_rows = pl.ds(pl.multiple_of(chip * 256, 256), 256)
    load_basis = pltpu.make_async_copy(basis_hbm.at[basis_rows], basis, load_sem.at[GROUPS + 1])
    load_basis.start()
    load_vel.wait()
    vel[...] = vel[...] * 0.5
    vel[2, 1] = -vel[2, 1]
    load_kappa.wait()
    load_rate.wait()

    def advance(k, g, now, new):
        e = k * GROUPS + g
        last = k == SECTIONS - 1
        x_copy(e, True).wait_recv()
        x_copy(e, False).wait_recv()
        y_copy(e, True).wait_recv()
        y_copy(e, False).wait_recv()

        wide = lax.broadcasted_iota(jnp.int32, halos.shape, 1)
        halos[...] = jnp.where(
            lax.rem(wide, 2) == 0,
            rolled(x_right[e].astype(F32), 127),
            rolled(x_left[e].astype(F32), 1),
        )

        for j in range(per):
            for z in range(2):
                now[g * per + j, z, pl.ds(7, 1), :] = y_recv[0, e, pl.ds(2 * j + z, 1), :]
                now[g * per + j, z, pl.ds(8 + ny, 1), :] = y_recv[1, e, pl.ds(2 * j + z, 1), :]

        @pl.loop(0, per, step=UNROLL)
        def _(j0):
            for i in range(UNROLL):
                j = j0 + (lax.rem(core + i, 2) if last else i)
                s = g * per + j
                kappa, rate = kappa_ref[s], rate_ref[s]
                middle = 1.0 - 6.0 * kappa - rate
                for z in range(2):
                    c = now[s, z, pl.ds(8, ny), :]
                    other = now[s, 1 - z, pl.ds(8, ny), :]
                    up = now[s, z, pl.ds(9, ny), :]
                    down = now[s, z, pl.ds(7, ny), :]
                    halo = rolled(halos[...], lax.rem(255 - 4 * j - 2 * z, 128))
                    east = jnp.where(lane == 127, halo, rolled(c, 127))
                    west = jnp.where(lane == 0, halo, rolled(c, 1))
                    result = (
                        c * (middle + rate * (1.0 / (1.0 + c * c)))
                        + kappa * ((east + west) + (up + down))
                        + (kappa - vel[2, z]) * other
                        - vel[0, z] * (east - west)
                        - vel[1, z] * (up - down)
                    )
                    if last:
                        evolved_ref[s, z] = result
                        cells = result.astype(BF16)
                        if i % 2 == 0:
                            pairs[s // 2, pl.ds(z * ny, ny), own_lanes] = cells
                        else:
                            outbox[s // 2, pl.ds(z * ny, ny), :] = cells
                    else:
                        new[s, z, pl.ds(8, ny), :] = result

        if not last:
            pack_edges(e + GROUPS, new, g * per)
            send_edges(e + GROUPS)

    buffers = (state, state_b)
    for k in range(SECTIONS - 1):

        @pl.loop(0, GROUPS)
        def _(g):
            advance(k, g, buffers[k % 2], buffers[(k + 1) % 2])

    load_basis.wait()

    def group_parts(g):
        pair_copy(g).wait_recv()
        send_parts(part_box, part_sum, 0, g * pairs_per, pairs_per, basis[...])

    @pl.loop(0, GROUPS)
    def _(g):
        advance(SECTIONS - 1, g, buffers[(SECTIONS - 1) % 2], None)
        pair_copy(g).start()

        @pl.when(g > 0)
        def _():
            group_parts(g - 1)

    group_parts(GROUPS - 1)

    def turned(at, cells):
        own_t[:, pl.ds(pl.multiple_of(at * 128, 128), 128)] = cells.T

    @pl.loop(0, half, step=2)
    def _(i):
        for k in range(2):
            turned(own_slot + i + k, pairs[i + k, :, own_lanes])
            turned(half - own_slot + i + k, outbox[i + k])

    proj[block(gx), :] = summed(part_box, part_sum, 0).astype(BF16)

    stride_a = 2 + 6 * core
    stride_b = 8 - 6 * core
    pos_a = lax.rem(gx // stride_a, 4)
    pos_b = lax.rem(gx // stride_b, 4)

    def device_at(a, b):
        return lax.rem(a, 4) * stride_a + lax.rem(b, 4) * stride_b + core

    def gather(held, use):
        def send(x, peer):
            pltpu.make_async_remote_copy(
                src_ref=held.at[block(x)],
                dst_ref=held.at[block(x)],
                send_sem=gs_sem,
                recv_sem=gr_sem.at[x],
                device_id={"gx": peer},
                device_id_type=MESH,
            ).start()

        def arrival(x):
            pltpu.make_async_copy(held.at[block(x)], held.at[block(x)], gr_sem.at[x]).wait()

        order = (1, 3, 2)
        for d in order:
            send(gx, device_at(pos_a + d, pos_b))
        for d in order:
            send(gx, device_at(pos_a, pos_b + d))
        send(gx, sibling)
        for d in order:
            x = device_at(pos_a + d, pos_b)
            arrival(x)
            for f in order:
                send(x, device_at(pos_a, pos_b + f))
            send(x, sibling)
        for d in (0, 1, 3, 2):
            for f in order:
                x = device_at(pos_a + d, pos_b + f)
                arrival(x)
                send(x, sibling)
        first = use(core)

        @pl.loop(0, half)
        def _(i):
            arrival(2 * i + 1 - core)

        second = use(1 - core)
        return first + second

    def gather_done(held):
        part = held.at[pl.ds(0, (ngx - 1) * 128)]
        pltpu.make_async_copy(part, part, gs_sem).wait()

    def span(c):
        return pl.ds(pl.multiple_of(c * (half * 128), half * 128), half * 128)

    part = gather(
        proj, lambda c: jnp.dot(own_t[:, span(c)], proj[span(c), :], preferred_element_type=F32)
    )

    image_part[gy] = part.astype(BF16)

    def image_copy(d):
        return pltpu.make_async_remote_copy(
            src_ref=image_part.at[gy],
            dst_ref=image_part.at[gy],
            send_sem=is_sem.at[d],
            recv_sem=ir_sem.at[gy],
            device_id={"gy": lax.rem(gy + d, ngy)},
            device_id_type=MESH,
        )

    for d in (1, 3, 2):
        image_copy(d).start()
    for d in (1, 3, 2):
        slot = lax.rem(gy + d, ngy)
        pltpu.make_async_copy(image_part.at[slot], image_part.at[slot], ir_sem.at[slot]).wait()
    image_own[...] = (image_part[0].astype(F32) + image_part[1].astype(F32)) + (
        image_part[2].astype(F32) + image_part[3].astype(F32)
    )
    image_pair[core] = image_own[...].astype(BF16)

    pair_image_copy = pltpu.make_async_remote_copy(
        src_ref=image_pair.at[core],
        dst_ref=image_pair.at[core],
        send_sem=ps_sem,
        recv_sem=pr_sem,
        device_id={"gx": sibling},
        device_id_type=MESH,
    )
    pair_image_copy.start()
    pair_image_copy.wait_recv()
    both = jnp.concatenate([image_pair[0], image_pair[1]], axis=0)

    gram_part[...] = lax.dot_general(both, both, (((0,), (0,)), ((), ())), preferred_element_type=F32)
    def share(y, c):
        return pl.ds(pl.multiple_of(y * 32 + c * 16, 16), 16)

    own_share = share(gy, core)
    gram_sum[chip] = gram_part[own_share, :]

    def gram_copy(d):
        return pltpu.make_async_remote_copy(
            src_ref=gram_part.at[own_share],
            dst_ref=gram_sum.at[chip],
            send_sem=ms_sem,
            recv_sem=mr_sem.at[chip],
            device_id={"gx": lax.rem(gx + 2 * d, ngx)},
            device_id_type=MESH,
        )

    @pl.loop(1, half)
    def _(d):
        gram_copy(d).start()

    @pl.loop(0, half, step=8)
    def _(i):
        send_parts(carry_box, carry_sum, 1, i, 8, both)

    @pl.loop(1, half)
    def _(d):
        slot = lax.rem(chip + half - d, half)
        pltpu.make_async_copy(gram_sum.at[slot], gram_sum.at[slot], mr_sem.at[slot]).wait()

    gram_all[own_share, :] = tree_sum([gram_sum[i] for i in range(half)])

    def rows_copy(d, c):
        return pltpu.make_async_remote_copy(
            src_ref=gram_all.at[own_share],
            dst_ref=gram_all.at[own_share],
            send_sem=ts_sem.at[d, c],
            recv_sem=tr_sem.at[gy, core],
            device_id={"gx": 2 * chip + lax.rem(core + c, 2), "gy": lax.rem(gy + d, ngy)},
            device_id_type=MESH,
        )

    others = ((1, 0), (3, 0), (2, 0), (0, 1), (1, 1), (3, 1), (2, 1))
    for d, c in others:
        rows_copy(d, c).start()
    for d, c in others:
        y, x = lax.rem(gy + d, ngy), lax.rem(core + c, 2)
        rows = gram_all.at[share(y, x)]
        pltpu.make_async_copy(rows, rows, tr_sem.at[y, x]).wait()

    mix_ref[...] = mixing(gram_all[...], 128.0 * ngx)
    carried_ref[...] = summed(carry_box, carry_sum, 1)
    image_ref[...] = image_own[pl.ds(pl.multiple_of(gy * 32, 32), 32), :]

    for d in range(2):
        pltpu.make_async_copy(x_send, x_send, xs_sem.at[d]).wait()
        pltpu.make_async_copy(y_send.at[d], y_send.at[d], ys_sem.at[d]).wait()
    pltpu.make_async_copy(outbox, outbox, cs_sem).wait()
    for which in range(2):
        sent = part_box.at[pl.ds(0, half - 1)]
        pltpu.make_async_copy(sent, sent, as_sem.at[which]).wait()
    gather_done(proj)
    pair_image_copy.wait_send()
    sent = gram_sum.at[pl.ds(0, half - 1)]
    pltpu.make_async_copy(sent, sent, ms_sem).wait()
    for d, c in others:
        rows_copy(d, c).wait_send()
    for d in (1, 3, 2):
        image_copy(d).wait_send()


def finish(scale, evolved_ref, mix_ref, carried_ref, image_ref, out_hbm, factor_ref, core_ref, sem):
    writing = pltpu.make_async_copy(evolved_ref, out_hbm, sem)
    writing.start()
    mix = mix_ref[...]
    factor_ref[...] = full_dot(image_ref[...], mix).astype(BF16)
    result = full_dot(carried_ref[...], mix) * scale
    ny = core_ref.shape[2]
    core_ref[0, 0] = result[:ny]
    core_ref[0, 1] = result[ny:]
    writing.wait()


def shards(initial_state, velocity, diffusivity, reaction_rate, start_basis):
    species, nz, ny, nx = initial_state.shape
    ngx, ngy = lax.axis_size("gx"), lax.axis_size("gy")
    rank = start_basis.shape[1]
    operands = (initial_state, velocity, diffusivity, reaction_rate, start_basis)
    exchanges = SECTIONS * GROUPS
    rows = 2 * species // GROUPS
    hbm = pl.BlockSpec(memory_space=pltpu.HBM)
    vmem = pl.BlockSpec(memory_space=pltpu.VMEM)
    dma = pltpu.SemaphoreType.DMA
    evolved, mix, carried, image = pl.pallas_call(
        kernel,
        out_shape=(
            jax.ShapeDtypeStruct(initial_state.shape, F32),
            jax.ShapeDtypeStruct((rank, rank), F32),
            jax.ShapeDtypeStruct((nz * ny, rank), F32),
            jax.ShapeDtypeStruct((nx // ngy, rank), F32),
        ),
        in_specs=[hbm] * 5,
        out_specs=(vmem,) * 4,
        scratch_shapes=[
            pltpu.VMEM((species, nz, ny + 16, nx), F32),
            pltpu.VMEM((species, nz, ny + 16, nx), F32),
            pltpu.VMEM((3, nz, ny, nx), F32),
            pltpu.SMEM((species,), F32),
            pltpu.SMEM((species,), F32),
            pltpu.VMEM((2 * nx, rank), BF16),
            pltpu.VMEM((ny, nx), F32),
            pltpu.VMEM((exchanges, ny, nx), BF16),
            pltpu.VMEM((exchanges, ny, nx), BF16),
            pltpu.VMEM((exchanges, ny, nx), BF16),
            pltpu.VMEM((2, exchanges, rows, nx), F32),
            pltpu.VMEM((2, exchanges, rows, nx), F32),
            pltpu.VMEM((species // 2, nz * ny, 2 * nx), BF16),
            pltpu.VMEM((species // 2, nz * ny, nx), BF16),
            pltpu.VMEM((nx, species * nz * ny), BF16),
            pltpu.VMEM((ngx // 2, nz * ny, rank), BF16),
            pltpu.VMEM((ngx // 2, nz * ny, rank), BF16),
            pltpu.VMEM((ngx // 2, nz * ny, rank), BF16),
            pltpu.VMEM((ngx // 2, nz * ny, rank), BF16),
            pltpu.VMEM((species * nz * ny, rank), BF16),
            pltpu.VMEM((ngy, nx, rank), BF16),
            pltpu.VMEM((2, nx, rank), BF16),
            pltpu.VMEM((nx, rank), F32),
            pltpu.VMEM((rank, rank), F32),
            pltpu.VMEM((ngx // 2, rank // (2 * ngy), rank), F32),
            pltpu.VMEM((rank, rank), F32),
            dma((GROUPS + 4,)),
            dma((2,)),
            dma((2, exchanges)),
            dma((2,)),
            dma((2, exchanges)),
            dma,
            dma((GROUPS,)),
            dma((2,)),
            dma((2, ngx // 2)),
            dma,
            dma((ngx,)),
            dma((ngy,)),
            dma((ngy,)),
            dma,
            dma,
            dma,
            dma((ngx // 2,)),
            dma((ngy, 2)),
            dma((ngy, 2)),
        ],
        compiler_params=pltpu.CompilerParams(
            collective_id=0, has_side_effects=True, vmem_limit_bytes=VMEM_LIMIT
        ),
    )(*(pltpu.with_memory_space_constraint(x, pltpu.HBM) for x in operands))
    return pl.pallas_call(
        functools.partial(finish, float(nx * ngx) ** -0.5),
        out_shape=(
            jax.ShapeDtypeStruct(initial_state.shape, F32),
            jax.ShapeDtypeStruct((nx // ngy, rank), BF16),
            jax.ShapeDtypeStruct((1, nz, ny, rank), F32),
        ),
        in_specs=[pl.BlockSpec(memory_space=pl.ANY), vmem, vmem, vmem],
        out_specs=(hbm, vmem, vmem),
        scratch_shapes=[dma],
        compiler_params=pltpu.CompilerParams(vmem_limit_bytes=8 << 20),
    )(evolved, mix, carried, image)


def solution(mesh):
    return jax.shard_map(
        shards,
        mesh=mesh,
        in_specs=(P(None, None, "gy", "gx"), P(None, None, "gy", "gx"), P(), P(), P()),
        out_specs=(P(None, None, "gy", "gx"), P(("gx", "gy"), None), P("gx", None, "gy", None)),
        check_vma=False,
    )
```

time: 76.9 us -> 70.9 us (0.922)
  Pallas kernels: 76.1 us -> 70.2 us
    pallas_call x1, Pallas kernels: 72.9 us -> 68.2 us  [shards(): pl.pallas_call(kernel, out_shape=(jax.ShapeDtypeStruct(initial_state.shap...]
    pallas_call x1, Pallas kernels: 3.17 us -> 1.97 us  [shards(): pl.pallas_call(functools.partial(finish, float(nx * ngx) ** (-0.5)), out_...]
where the time goes in v2:
time: 70.9 us; the launch traced here: 70.8 us
  Pallas kernels  70.2 us (99%)
    pallas_call x1, Pallas kernels, shards(): pl.pallas_call(kernel, out_shape=(jax.ShapeDtypeStruct(initial_state.shap...  68.2 us
    pallas_call x1, Pallas kernels, shards(): pl.pallas_call(functools.partial(finish, float(nx * ngx) ** (-0.5)), out_...  1.97 us

profile of v2, /device:TPU:1, one launch (start us, length us, event | category | flops | bytes accessed | tf_op | source)
XLA Modules:
  0.0 70.8 jit_solution(4508996667270160460)
XLA Ops:
  0.6 68.2 %shard_map.76 = (f32[32,2,64,128]{3,2,1,0:T(8,128)S(1)}, f32[128,128]{1,0:T(8,128)S(1)}, f32[128,128]{1,0:T(8,128)S(1)}, f32[32,128]{1,0:T(8,128)S(1)}) custom-call(f32[32,2,64,128]{3,2,1,0:T(8,128)} %init_hbm.1, f32[3,2,64,128]{3,2,1,0:T(8,128)} %vel_hbm.1, f32[32]{0:T(128)} %kappa_hbm.1, f32[32]{0:T(128)} %rate_hbm.1, bf16[4096,128]{1,0:T(8,128)(2,1)} %basis_hbm.1), custom_call_target="tpu_custom_call" | custom-call | tf_op jit(solution)/shard_map/pallas_call | solution.py:496
  68.8 2.0 %shard_map.77 = (f32[32,2,64,128]{3,2,1,0:T(8,128)}, bf16[32,128]{1,0:T(8,128)(2,1)}, f32[1,2,64,128]{3,2,1,0:T(8,128)}) custom-call(f32[32,2,64,128]{3,2,1,0:T(8,128)S(1)} %get-tuple-element.7.evolved_ref, f32[128,128]{1,0:T(8,128)S(1)} %get-tuple-element.8.mix_ref, f32[128,128]{1,0:T(8,128)S(1)} %get-tuple-element.9.carried_ref, ...), custom_call_target="tpu_custom_call" | custom-call | tf_op jit(solution)/shard_map/pallas_call | solution.py:557

commit v3 on v2

--- a/solution.py
+++ b/solution.py
@@ -61,9 +61,9 @@
 def kernel(
     init_hbm, vel_hbm, kappa_hbm, rate_hbm, basis_hbm,
     evolved_ref, mix_ref, carried_ref, image_ref,
-    state, state_b, vel, kappa_ref, rate_ref, basis, halos, x_send, x_left, x_right, y_send, y_recv,
-    pairs, outbox, own_t, part_box, part_sum, carry_box, carry_sum, proj, image_part, image_pair, image_own, gram_part, gram_sum, gram_all,
-    load_sem, xs_sem, xr_sem, ys_sem, yr_sem, cs_sem, cr_sem, as_sem, ar_sem, gs_sem, gr_sem, is_sem, ir_sem, ps_sem, pr_sem, ms_sem, mr_sem, ts_sem, tr_sem,
+    state, state_b, vel, kappa_ref, rate_ref, basis, halos, x_send, x_recv, y_send, y_recv,
+    pairs, outbox, pairs_t, part_box, part_sum, carry_box, carry_sum, proj, half_send, half_recv, image_part, image_pair, image_own, gram_part, gram_sum, gram_all,
+    load_sem, xs_sem, xr_sem, ys_sem, yr_sem, cs_sem, cr_sem, as_sem, ar_sem, gs_sem, gr_sem, is_sem, ir_sem, hs_sem, hr_sem, ps_sem, pr_sem, ms_sem, mr_sem, ts_sem, tr_sem,
 ):
     species = state.shape[0]
     ny = state.shape[2] - 16
@@ -77,27 +77,15 @@
     chip = gx // 2
     sibling = gx + 1 - 2 * core
     own_lanes = pl.ds(pl.multiple_of(core * 128, 128), 128)
-    own_slot = core * half
     pairs_per = per // 2
     lane = lax.broadcasted_iota(jnp.int32, (ny, 128), 1)
     pair = lane // 2
 
-    def block(x):
-        at = lax.rem(x, 2) * half + x // 2
-        return pl.ds(pl.multiple_of(at * 128, 128), 128)
-
-    def load_state(g):
-        return pltpu.make_async_copy(
-            init_hbm.at[pl.ds(g * per, per)],
-            state.at[pl.ds(g * per, per), :, pl.ds(8, ny), :],
-            load_sem.at[g],
-        )
-
-    load_vel = pltpu.make_async_copy(vel_hbm, vel, load_sem.at[GROUPS])
-    load_kappa = pltpu.make_async_copy(kappa_hbm, kappa_ref, load_sem.at[GROUPS + 2])
-    load_rate = pltpu.make_async_copy(rate_hbm, rate_ref, load_sem.at[GROUPS + 3])
-    for g in range(GROUPS):
-        load_state(g).start()
+    load_state = pltpu.make_async_copy(init_hbm, state.at[:, :, pl.ds(8, ny), :], load_sem.at[0])
+    load_vel = pltpu.make_async_copy(vel_hbm, vel, load_sem.at[1])
+    load_kappa = pltpu.make_async_copy(kappa_hbm, kappa_ref, load_sem.at[2])
+    load_rate = pltpu.make_async_copy(rate_hbm, rate_ref, load_sem.at[3])
+    load_state.start()
     load_kappa.start()
     load_rate.start()
     load_vel.start()
@@ -121,9 +109,9 @@
     def x_copy(e, to_left):
         return pltpu.make_async_remote_copy(
             src_ref=x_send.at[e],
-            dst_ref=(x_right if to_left else x_left).at[e],
+            dst_ref=x_recv.at[e, int(to_left)],
             send_sem=xs_sem.at[int(to_left)],
-            recv_sem=xr_sem.at[int(to_left), e],
+            recv_sem=xr_sem.at[e],
             device_id={"gx": left if to_left else right},
             device_id_type=MESH,
         )
@@ -132,9 +120,9 @@
         d = int(to_south)
         return pltpu.make_async_remote_copy(
             src_ref=y_send.at[d, e],
-            dst_ref=y_recv.at[d, e],
+            dst_ref=y_recv.at[e, d],
             send_sem=ys_sem.at[d],
-            recv_sem=yr_sem.at[d, e],
+            recv_sem=yr_sem.at[e],
             device_id={"gy": south if to_south else north},
             device_id_type=MESH,
         )
@@ -154,7 +142,7 @@
             src_ref=box.at[i],
             dst_ref=total.at[chip],
             send_sem=as_sem.at[which],
-            recv_sem=ar_sem.at[which, chip],
+            recv_sem=ar_sem.at[which],
             device_id={"gx": 2 * i + core},
             device_id_type=MESH,
         )
@@ -170,12 +158,12 @@
             def _():
                 part_copy(box, total, which, i).start()
 
+    def all_of(ref, count):
+        return ref.at[pl.ds(0, count)]
+
     def summed(box, total, which):
-        @pl.loop(1, half)
-        def _(d):
-            slot = lax.rem(chip + half - d, half)
-            pltpu.make_async_copy(total.at[slot], total.at[slot], ar_sem.at[which, slot]).wait()
-
+        arrived = all_of(total, half - 1)
+        pltpu.make_async_copy(arrived, arrived, ar_sem.at[which]).wait()
         total[chip] = box[chip]
         return tree_sum([total[i].astype(F32) for i in range(half)])
 
@@ -194,8 +182,7 @@
         y_copy(e, True).start()
         y_copy(e, False).start()
 
-    for g in range(GROUPS):
-        load_state(g).wait()
+    load_state.wait()
 
     @pl.loop(0, GROUPS)
     def _(g):
@@ -208,7 +195,7 @@
         send_edges(g)
 
     basis_rows = pl.ds(pl.multiple_of(chip * 256, 256), 256)
-    load_basis = pltpu.make_async_copy(basis_hbm.at[basis_rows], basis, load_sem.at[GROUPS + 1])
+    load_basis = pltpu.make_async_copy(basis_hbm.at[basis_rows], basis, load_sem.at[4])
     load_basis.start()
     load_vel.wait()
     vel[...] = vel[...] * 0.5
@@ -219,22 +206,20 @@
     def advance(k, g, now, new):
         e = k * GROUPS + g
         last = k == SECTIONS - 1
-        x_copy(e, True).wait_recv()
-        x_copy(e, False).wait_recv()
-        y_copy(e, True).wait_recv()
-        y_copy(e, False).wait_recv()
+        pltpu.make_async_copy(x_recv.at[e], x_recv.at[e], xr_sem.at[e]).wait()
+        pltpu.make_async_copy(y_recv.at[e], y_recv.at[e], yr_sem.at[e]).wait()
 
         wide = lax.broadcasted_iota(jnp.int32, halos.shape, 1)
         halos[...] = jnp.where(
             lax.rem(wide, 2) == 0,
-            rolled(x_right[e].astype(F32), 127),
-            rolled(x_left[e].astype(F32), 1),
+            rolled(x_recv[e, 1].astype(F32), 127),
+            rolled(x_recv[e, 0].astype(F32), 1),
         )
 
         for j in range(per):
             for z in range(2):
-                now[g * per + j, z, pl.ds(7, 1), :] = y_recv[0, e, pl.ds(2 * j + z, 1), :]
-                now[g * per + j, z, pl.ds(8 + ny, 1), :] = y_recv[1, e, pl.ds(2 * j + z, 1), :]
+                now[g * per + j, z, pl.ds(7, 1), :] = y_recv[e, 0, pl.ds(2 * j + z, 1), :]
+                now[g * per + j, z, pl.ds(8 + ny, 1), :] = y_recv[e, 1, pl.ds(2 * j + z, 1), :]
 
         @pl.loop(0, per, step=UNROLL)
         def _(j0):
@@ -296,75 +281,99 @@
 
     group_parts(GROUPS - 1)
 
-    def turned(at, cells):
-        own_t[:, pl.ds(pl.multiple_of(at * 128, 128), 128)] = cells.T
-
     @pl.loop(0, half, step=2)
     def _(i):
         for k in range(2):
-            turned(own_slot + i + k, pairs[i + k, :, own_lanes])
-            turned(half - own_slot + i + k, outbox[i + k])
-
-    proj[block(gx), :] = summed(part_box, part_sum, 0).astype(BF16)
-
-    stride_a = 2 + 6 * core
-    stride_b = 8 - 6 * core
-    pos_a = lax.rem(gx // stride_a, 4)
-    pos_b = lax.rem(gx // stride_b, 4)
-
-    def device_at(a, b):
-        return lax.rem(a, 4) * stride_a + lax.rem(b, 4) * stride_b + core
-
-    def gather(held, use):
-        def send(x, peer):
-            pltpu.make_async_remote_copy(
-                src_ref=held.at[block(x)],
-                dst_ref=held.at[block(x)],
-                send_sem=gs_sem,
-                recv_sem=gr_sem.at[x],
-                device_id={"gx": peer},
-                device_id_type=MESH,
-            ).start()
-
-        def arrival(x):
-            pltpu.make_async_copy(held.at[block(x)], held.at[block(x)], gr_sem.at[x]).wait()
-
-        order = (1, 3, 2)
+            pairs_t[:, pl.ds(pl.multiple_of((i + k) * 128, 128), 128)] = pairs[i + k].T
+
+    def block(x):
+        return pl.ds(pl.multiple_of(x // 2 * 128, 128), 128)
+
+    plane = gx // per
+    across = pairs_per
+
+    def in_plane(x, d):
+        return x // per * per + lax.rem(x + 2 * d, per)
+
+    def other_plane(x, d):
+        return lax.rem(x + d * per, ngx)
+
+    def send(x, peer):
+        pltpu.make_async_remote_copy(
+            src_ref=proj.at[block(x)],
+            dst_ref=proj.at[block(x)],
+            send_sem=gs_sem,
+            recv_sem=gr_sem.at[x // 2],
+            device_id={"gx": peer},
+            device_id_type=MESH,
+        ).start()
+
+    def arrival(x):
+        pltpu.make_async_copy(proj.at[block(x)], proj.at[block(x)], gr_sem.at[x // 2]).wait()
+
+    order = (1, 3, 2)
+
+    @pl.loop(0, GROUPS)
+    def _(p):
+        @pl.when(p == plane)
+        def _():
+            proj[block(gx), :] = summed(part_box, part_sum, 0).astype(BF16)
+
+            @pl.when(core == 0)
+            def _():
+                for d in order:
+                    send(gx, in_plane(gx, d))
+                for d in order:
+                    send(gx, other_plane(gx, d))
+
+            @pl.when(core == 1)
+            def _():
+                for d in order:
+                    send(gx, other_plane(gx, d))
+                for d in order:
+                    send(gx, in_plane(gx, d))
+
+        @pl.when((p != plane) & (core == 1))
+        def _():
+            x = p * per + lax.rem(gx, per)
+            arrival(x)
+            for d in order:
+                send(x, in_plane(gx, d))
+
+    @pl.when(core == 0)
+    def _():
         for d in order:
-            send(gx, device_at(pos_a + d, pos_b))
-        for d in order:
-            send(gx, device_at(pos_a, pos_b + d))
-        send(gx, sibling)
-        for d in order:
-            x = device_at(pos_a + d, pos_b)
+            x = in_plane(gx, d)
             arrival(x)
             for f in order:
-                send(x, device_at(pos_a, pos_b + f))
-            send(x, sibling)
-        for d in (0, 1, 3, 2):
-            for f in order:
-                x = device_at(pos_a + d, pos_b + f)
-                arrival(x)
-                send(x, sibling)
-        first = use(core)
-
-        @pl.loop(0, half)
-        def _(i):
-            arrival(2 * i + 1 - core)
-
-        second = use(1 - core)
-        return first + second
-
-    def gather_done(held):
-        part = held.at[pl.ds(0, (ngx - 1) * 128)]
-        pltpu.make_async_copy(part, part, gs_sem).wait()
-
-    def span(c):
-        return pl.ds(pl.multiple_of(c * (half * 128), half * 128), half * 128)
-
-    part = gather(
-        proj, lambda c: jnp.dot(own_t[:, span(c)], proj[span(c), :], preferred_element_type=F32)
+                send(x, other_plane(gx, f))
+        for f in order:
+            for d in range(across):
+                arrival(in_plane(other_plane(gx, f), d))
+
+    @pl.when(core == 1)
+    def _():
+        for d in order:
+            for f in range(GROUPS):
+                arrival(other_plane(in_plane(gx, d), f))
+
+    def image_half(c):
+        rows = pl.ds(pl.multiple_of(c * 128, 128), 128)
+        return jnp.dot(pairs_t[rows, :], proj[...], preferred_element_type=F32)
+
+    half_send[...] = image_half(1 - core).astype(BF16)
+    half_copy = pltpu.make_async_remote_copy(
+        src_ref=half_send,
+        dst_ref=half_recv,
+        send_sem=hs_sem,
+        recv_sem=hr_sem,
+        device_id={"gx": sibling},
+        device_id_type=MESH,
     )
+    half_copy.start()
+    part = image_half(core)
+    half_copy.wait_recv()
+    part = part + half_recv[...].astype(F32)
 
     image_part[gy] = part.astype(BF16)
 
@@ -372,17 +381,16 @@
         return pltpu.make_async_remote_copy(
             src_ref=image_part.at[gy],
             dst_ref=image_part.at[gy],
-            send_sem=is_sem.at[d],
-            recv_sem=ir_sem.at[gy],
+            send_sem=is_sem,
+            recv_sem=ir_sem,
             device_id={"gy": lax.rem(gy + d, ngy)},
             device_id_type=MESH,
         )
 
     for d in (1, 3, 2):
         image_copy(d).start()
-    for d in (1, 3, 2):
-        slot = lax.rem(gy + d, ngy)
-        pltpu.make_async_copy(image_part.at[slot], image_part.at[slot], ir_sem.at[slot]).wait()
+    arrived = all_of(image_part, ngy - 1)
+    pltpu.make_async_copy(arrived, arrived, ir_sem).wait()
     image_own[...] = (image_part[0].astype(F32) + image_part[1].astype(F32)) + (
         image_part[2].astype(F32) + image_part[3].astype(F32)
     )
@@ -412,7 +420,7 @@
             src_ref=gram_part.at[own_share],
             dst_ref=gram_sum.at[chip],
             send_sem=ms_sem,
-            recv_sem=mr_sem.at[chip],
+            recv_sem=mr_sem,
             device_id={"gx": lax.rem(gx + 2 * d, ngx)},
             device_id_type=MESH,
         )
@@ -425,10 +433,8 @@
     def _(i):
         send_parts(carry_box, carry_sum, 1, i, 8, both)
 
-    @pl.loop(1, half)
-    def _(d):
-        slot = lax.rem(chip + half - d, half)
-        pltpu.make_async_copy(gram_sum.at[slot], gram_sum.at[slot], mr_sem.at[slot]).wait()
+    arrived = all_of(gram_sum, half - 1)
+    pltpu.make_async_copy(arrived, arrived, mr_sem).wait()
 
     gram_all[own_share, :] = tree_sum([gram_sum[i] for i in range(half)])
 
@@ -436,8 +442,8 @@
         return pltpu.make_async_remote_copy(
             src_ref=gram_all.at[own_share],
             dst_ref=gram_all.at[own_share],
-            send_sem=ts_sem.at[d, c],
-            recv_sem=tr_sem.at[gy, core],
+            send_sem=ts_sem,
+            recv_sem=tr_sem,
             device_id={"gx": 2 * chip + lax.rem(core + c, 2), "gy": lax.rem(gy + d, ngy)},
             device_id_type=MESH,
         )
@@ -445,10 +451,8 @@
     others = ((1, 0), (3, 0), (2, 0), (0, 1), (1, 1), (3, 1), (2, 1))
     for d, c in others:
         rows_copy(d, c).start()
-    for d, c in others:
-        y, x = lax.rem(gy + d, ngy), lax.rem(core + c, 2)
-        rows = gram_all.at[share(y, x)]
-        pltpu.make_async_copy(rows, rows, tr_sem.at[y, x]).wait()
+    arrived = all_of(gram_all, 16 * len(others))
+    pltpu.make_async_copy(arrived, arrived, tr_sem).wait()
 
     mix_ref[...] = mixing(gram_all[...], 128.0 * ngx)
     carried_ref[...] = summed(carry_box, carry_sum, 1)
@@ -461,14 +465,16 @@
     for which in range(2):
         sent = part_box.at[pl.ds(0, half - 1)]
         pltpu.make_async_copy(sent, sent, as_sem.at[which]).wait()
-    gather_done(proj)
+    sent = all_of(proj, (half - 1) * 128)
+    pltpu.make_async_copy(sent, sent, gs_sem).wait()
+    half_copy.wait_send()
     pair_image_copy.wait_send()
     sent = gram_sum.at[pl.ds(0, half - 1)]
     pltpu.make_async_copy(sent, sent, ms_sem).wait()
-    for d, c in others:
-        rows_copy(d, c).wait_send()
-    for d in (1, 3, 2):
-        image_copy(d).wait_send()
+    sent = all_of(gram_all, 16 * len(others))
+    pltpu.make_async_copy(sent, sent, ts_sem).wait()
+    sent = all_of(image_part, ngy - 1)
+    pltpu.make_async_copy(sent, sent, is_sem).wait()
 
 
 def finish(scale, evolved_ref, mix_ref, carried_ref, image_ref, out_hbm, factor_ref, core_ref, sem):
@@ -512,43 +518,46 @@
             pltpu.VMEM((2 * nx, rank), BF16),
             pltpu.VMEM((ny, nx), F32),
             pltpu.VMEM((exchanges, ny, nx), BF16),
-            pltpu.VMEM((exchanges, ny, nx), BF16),
-            pltpu.VMEM((exchanges, ny, nx), BF16),
+            pltpu.VMEM((exchanges, 2, ny, nx), BF16),
             pltpu.VMEM((2, exchanges, rows, nx), F32),
-            pltpu.VMEM((2, exchanges, rows, nx), F32),
+            pltpu.VMEM((exchanges, 2, rows, nx), F32),
             pltpu.VMEM((species // 2, nz * ny, 2 * nx), BF16),
             pltpu.VMEM((species // 2, nz * ny, nx), BF16),
-            pltpu.VMEM((nx, species * nz * ny), BF16),
+            pltpu.VMEM((2 * nx, species // 2 * nz * ny), BF16),
             pltpu.VMEM((ngx // 2, nz * ny, rank), BF16),
             pltpu.VMEM((ngx // 2, nz * ny, rank), BF16),
             pltpu.VMEM((ngx // 2, nz * ny, rank), BF16),
             pltpu.VMEM((ngx // 2, nz * ny, rank), BF16),
-            pltpu.VMEM((species * nz * ny, rank), BF16),
+            pltpu.VMEM((species // 2 * nz * ny, rank), BF16),
+            pltpu.VMEM((nx, rank), BF16),
+            pltpu.VMEM((nx, rank), BF16),
             pltpu.VMEM((ngy, nx, rank), BF16),
             pltpu.VMEM((2, nx, rank), BF16),
             pltpu.VMEM((nx, rank), F32),
             pltpu.VMEM((rank, rank), F32),
             pltpu.VMEM((ngx // 2, rank // (2 * ngy), rank), F32),
             pltpu.VMEM((rank, rank), F32),
-            dma((GROUPS + 4,)),
+            dma((5,)),
             dma((2,)),
-            dma((2, exchanges)),
+            dma((exchanges,)),
             dma((2,)),
-            dma((2, exchanges)),
+            dma((exchanges,)),
             dma,
             dma((GROUPS,)),
             dma((2,)),
-            dma((2, ngx // 2)),
-            dma,
-            dma((ngx,)),
-            dma((ngy,)),
-            dma((ngy,)),
-            dma,
-            dma,
+            dma((2,)),
             dma,
             dma((ngx // 2,)),
-            dma((ngy, 2)),
-            dma((ngy, 2)),
+            dma,
+            dma,
+            dma,
+            dma,
+            dma,
+            dma,
+            dma,
+            dma,
+            dma,
+            dma,
         ],
         compiler_params=pltpu.CompilerParams(
             collective_id=0, has_side_effects=True, vmem_limit_bytes=VMEM_LIMIT

time: 70.9 us -> 69.8 us (0.984)
  Pallas kernels: 70.2 us -> 69 us
    pallas_call x1, Pallas kernels: 68.2 us -> 67.1 us  [shards(): pl.pallas_call(kernel, out_shape=(jax.ShapeDtypeStruct(initial_state.shap...]
where the time goes in v3:
time: 69.8 us; the launch traced here: 69.7 us
  Pallas kernels  69 us (99%)
    pallas_call x1, Pallas kernels, shards(): pl.pallas_call(kernel, out_shape=(jax.ShapeDtypeStruct(initial_state.shap...  67.1 us
    pallas_call x1, Pallas kernels, shards(): pl.pallas_call(functools.partial(finish, float(nx * ngx) ** (-0.5)), out_...  1.97 us

profile of v3, /device:TPU:1, one launch (start us, length us, event | category | flops | bytes accessed | tf_op | source)
XLA Modules:
  0.0 69.7 jit_solution(13648355126493413905)
XLA Ops:
  0.6 67.1 %shard_map.76 = (f32[32,2,64,128]{3,2,1,0:T(8,128)S(1)}, f32[128,128]{1,0:T(8,128)S(1)}, f32[128,128]{1,0:T(8,128)S(1)}, f32[32,128]{1,0:T(8,128)S(1)}) custom-call(f32[32,2,64,128]{3,2,1,0:T(8,128)} %init_hbm.1, f32[3,2,64,128]{3,2,1,0:T(8,128)} %vel_hbm.1, f32[32]{0:T(128)} %kappa_hbm.1, f32[32]{0:T(128)} %rate_hbm.1, bf16[4096,128]{1,0:T(8,128)(2,1)} %basis_hbm.1), custom_call_target="tpu_custom_call" | custom-call | tf_op jit(solution)/shard_map/pallas_call | solution.py:502
  67.7 2.0 %shard_map.77 = (f32[32,2,64,128]{3,2,1,0:T(8,128)}, bf16[32,128]{1,0:T(8,128)(2,1)}, f32[1,2,64,128]{3,2,1,0:T(8,128)}) custom-call(f32[32,2,64,128]{3,2,1,0:T(8,128)S(1)} %get-tuple-element.7.evolved_ref, f32[128,128]{1,0:T(8,128)S(1)} %get-tuple-element.8.mix_ref, f32[128,128]{1,0:T(8,128)S(1)} %get-tuple-element.9.carried_ref, ...), custom_call_target="tpu_custom_call" | custom-call | tf_op jit(solution)/shard_map/pallas_call | solution.py:566

commit v4 on v3

--- a/solution.py
+++ b/solution.py
@@ -60,7 +60,7 @@
 
 def kernel(
     init_hbm, vel_hbm, kappa_hbm, rate_hbm, basis_hbm,
-    evolved_ref, mix_ref, carried_ref, image_ref,
+    evolved_ref, gram_ref, carried_ref, image_ref,
     state, state_b, vel, kappa_ref, rate_ref, basis, halos, x_send, x_recv, y_send, y_recv,
     pairs, outbox, pairs_t, part_box, part_sum, carry_box, carry_sum, proj, half_send, half_recv, image_part, image_pair, image_own, gram_part, gram_sum, gram_all,
     load_sem, xs_sem, xr_sem, ys_sem, yr_sem, cs_sem, cr_sem, as_sem, ar_sem, gs_sem, gr_sem, is_sem, ir_sem, hs_sem, hr_sem, ps_sem, pr_sem, ms_sem, mr_sem, ts_sem, tr_sem,
@@ -85,20 +85,10 @@
     load_vel = pltpu.make_async_copy(vel_hbm, vel, load_sem.at[1])
     load_kappa = pltpu.make_async_copy(kappa_hbm, kappa_ref, load_sem.at[2])
     load_rate = pltpu.make_async_copy(rate_hbm, rate_ref, load_sem.at[3])
-    load_state.start()
-    load_kappa.start()
-    load_rate.start()
-    load_vel.start()
-
     barrier = pltpu.get_barrier_semaphore()
-
-    @pl.loop(1, half)
-    def _(d):
-        peer = lax.rem(gx + 2 * d, ngx)
-        pl.semaphore_signal(barrier, 1, device_id={"gx": peer}, device_id_type=MESH)
-
     for peer in (left, right):
         pl.semaphore_signal(barrier, 1, device_id={"gx": peer}, device_id_type=MESH)
+    load_state.start()
 
     @pl.loop(1, ngy)
     def _(d):
@@ -106,6 +96,15 @@
         pl.semaphore_signal(barrier, 1, device_id={"gy": peer}, device_id_type=MESH)
         pl.semaphore_signal(barrier, 1, device_id={"gx": sibling, "gy": peer}, device_id_type=MESH)
 
+    @pl.loop(1, half)
+    def _(d):
+        peer = lax.rem(gx + 2 * d, ngx)
+        pl.semaphore_signal(barrier, 1, device_id={"gx": peer}, device_id_type=MESH)
+
+    load_kappa.start()
+    load_rate.start()
+    load_vel.start()
+
     def x_copy(e, to_left):
         return pltpu.make_async_remote_copy(
             src_ref=x_send.at[e],
@@ -147,16 +146,10 @@
             device_id_type=MESH,
         )
 
-    def send_parts(box, total, which, first, count, rows):
+    def make_parts(box, first, count, rows):
         cells = pairs[pl.ds(first, count)].reshape(count * pairs.shape[1], pairs.shape[2])
         parts = jnp.dot(cells, rows, preferred_element_type=F32).astype(BF16)
         box[pl.ds(first, count)] = parts.reshape(count, *box.shape[1:])
-
-        @pl.loop(first, first + count)
-        def _(i):
-            @pl.when(i != chip)
-            def _():
-                part_copy(box, total, which, i).start()
 
     def all_of(ref, count):
         return ref.at[pl.ds(0, count)]
@@ -221,37 +214,51 @@
                 now[g * per + j, z, pl.ds(7, 1), :] = y_recv[e, 0, pl.ds(2 * j + z, 1), :]
                 now[g * per + j, z, pl.ds(8 + ny, 1), :] = y_recv[e, 1, pl.ds(2 * j + z, 1), :]
 
-        @pl.loop(0, per, step=UNROLL)
-        def _(j0):
-            for i in range(UNROLL):
-                j = j0 + (lax.rem(core + i, 2) if last else i)
-                s = g * per + j
-                kappa, rate = kappa_ref[s], rate_ref[s]
-                middle = 1.0 - 6.0 * kappa - rate
-                for z in range(2):
-                    c = now[s, z, pl.ds(8, ny), :]
-                    other = now[s, 1 - z, pl.ds(8, ny), :]
-                    up = now[s, z, pl.ds(9, ny), :]
-                    down = now[s, z, pl.ds(7, ny), :]
-                    halo = rolled(halos[...], lax.rem(255 - 4 * j - 2 * z, 128))
-                    east = jnp.where(lane == 127, halo, rolled(c, 127))
-                    west = jnp.where(lane == 0, halo, rolled(c, 1))
-                    result = (
-                        c * (middle + rate * (1.0 / (1.0 + c * c)))
-                        + kappa * ((east + west) + (up + down))
-                        + (kappa - vel[2, z]) * other
-                        - vel[0, z] * (east - west)
-                        - vel[1, z] * (up - down)
-                    )
-                    if last:
-                        evolved_ref[s, z] = result
-                        cells = result.astype(BF16)
-                        if i % 2 == 0:
-                            pairs[s // 2, pl.ds(z * ny, ny), own_lanes] = cells
-                        else:
-                            outbox[s // 2, pl.ds(z * ny, ny), :] = cells
+        def step(j, box):
+            s = g * per + j
+            kappa, rate = kappa_ref[s], rate_ref[s]
+            middle = 1.0 - 6.0 * kappa - rate
+            for z in range(2):
+                c = now[s, z, pl.ds(8, ny), :]
+                other = now[s, 1 - z, pl.ds(8, ny), :]
+                up = now[s, z, pl.ds(9, ny), :]
+                down = now[s, z, pl.ds(7, ny), :]
+                halo = rolled(halos[...], lax.rem(255 - 4 * j - 2 * z, 128))
+                east = jnp.where(lane == 127, halo, rolled(c, 127))
+                west = jnp.where(lane == 0, halo, rolled(c, 1))
+                result = (
+                    c * (middle + rate * (1.0 / (1.0 + c * c)))
+                    + kappa * ((east + west) + (up + down))
+                    + (kappa - vel[2, z]) * other
+                    - vel[0, z] * (east - west)
+                    - vel[1, z] * (up - down)
+                )
+                if last:
+                    evolved_ref[s, z] = result
+                    cells = result.astype(BF16)
+                    if box is pairs:
+                        pairs[s // 2, pl.ds(z * ny, ny), own_lanes] = cells
                     else:
-                        new[s, z, pl.ds(8, ny), :] = result
+                        outbox[s // 2, pl.ds(z * ny, ny), :] = cells
+                else:
+                    new[s, z, pl.ds(8, ny), :] = result
+
+        if last:
+            for box, parity in ((outbox, 1 - core), (pairs, core)):
+
+                @pl.loop(0, per, step=2 * UNROLL)
+                def _(j):
+                    for i in range(UNROLL):
+                        step(j + 2 * i + parity, box)
+
+                if box is outbox:
+                    pair_copy(g).start()
+        else:
+
+            @pl.loop(0, per, step=UNROLL)
+            def _(j):
+                for i in range(UNROLL):
+                    step(j + i, None)
 
         if not last:
             pack_edges(e + GROUPS, new, g * per)
@@ -268,13 +275,19 @@
 
     def group_parts(g):
         pair_copy(g).wait_recv()
-        send_parts(part_box, part_sum, 0, g * pairs_per, pairs_per, basis[...])
+        make_parts(part_box, g * pairs_per, pairs_per, basis[...])
+
+        @pl.loop(0, pairs_per)
+        def _(d):
+            i = g * pairs_per + lax.rem(chip + d, pairs_per)
+
+            @pl.when(i != chip)
+            def _():
+                part_copy(part_box, part_sum, 0, i).start()
 
     @pl.loop(0, GROUPS)
     def _(g):
         advance(SECTIONS - 1, g, buffers[(SECTIONS - 1) % 2], None)
-        pair_copy(g).start()
-
         @pl.when(g > 0)
         def _():
             group_parts(g - 1)
@@ -290,7 +303,6 @@
         return pl.ds(pl.multiple_of(x // 2 * 128, 128), 128)
 
     plane = gx // per
-    across = pairs_per
 
     def in_plane(x, d):
         return x // per * per + lax.rem(x + 2 * d, per)
@@ -313,49 +325,25 @@
 
     order = (1, 3, 2)
 
+    proj[block(gx), :] = summed(part_box, part_sum, 0).astype(BF16)
+
+    for d in order:
+        send(gx, other_plane(gx, d))
+    for d in order:
+        send(gx, in_plane(gx, d))
+
     @pl.loop(0, GROUPS)
     def _(p):
-        @pl.when(p == plane)
-        def _():
-            proj[block(gx), :] = summed(part_box, part_sum, 0).astype(BF16)
-
-            @pl.when(core == 0)
-            def _():
-                for d in order:
-                    send(gx, in_plane(gx, d))
-                for d in order:
-                    send(gx, other_plane(gx, d))
-
-            @pl.when(core == 1)
-            def _():
-                for d in order:
-                    send(gx, other_plane(gx, d))
-                for d in order:
-                    send(gx, in_plane(gx, d))
-
-        @pl.when((p != plane) & (core == 1))
+        @pl.when(p != plane)
         def _():
             x = p * per + lax.rem(gx, per)
             arrival(x)
             for d in order:
                 send(x, in_plane(gx, d))
 
-    @pl.when(core == 0)
-    def _():
-        for d in order:
-            x = in_plane(gx, d)
-            arrival(x)
-            for f in order:
-                send(x, other_plane(gx, f))
-        for f in order:
-            for d in range(across):
-                arrival(in_plane(other_plane(gx, f), d))
-
-    @pl.when(core == 1)
-    def _():
-        for d in order:
-            for f in range(GROUPS):
-                arrival(other_plane(in_plane(gx, d), f))
+    for d in order:
+        for f in range(GROUPS):
+            arrival(other_plane(in_plane(gx, d), f))
 
     def image_half(c):
         rows = pl.ds(pl.multiple_of(c * 128, 128), 128)
@@ -431,7 +419,11 @@
 
     @pl.loop(0, half, step=8)
     def _(i):
-        send_parts(carry_box, carry_sum, 1, i, 8, both)
+        make_parts(carry_box, i, 8, both)
+
+    @pl.loop(1, half)
+    def _(d):
+        part_copy(carry_box, carry_sum, 1, lax.rem(chip + d, half)).start()
 
     arrived = all_of(gram_sum, half - 1)
     pltpu.make_async_copy(arrived, arrived, mr_sem).wait()
@@ -454,7 +446,7 @@
     arrived = all_of(gram_all, 16 * len(others))
     pltpu.make_async_copy(arrived, arrived, tr_sem).wait()
 
-    mix_ref[...] = mixing(gram_all[...], 128.0 * ngx)
+    gram_ref[...] = gram_all[...]
     carried_ref[...] = summed(carry_box, carry_sum, 1)
     image_ref[...] = image_own[pl.ds(pl.multiple_of(gy * 32, 32), 32), :]
 
@@ -477,12 +469,12 @@
     pltpu.make_async_copy(sent, sent, is_sem).wait()
 
 
-def finish(scale, evolved_ref, mix_ref, carried_ref, image_ref, out_hbm, factor_ref, core_ref, sem):
+def finish(count, evolved_ref, gram_ref, carried_ref, image_ref, out_hbm, factor_ref, core_ref, sem):
     writing = pltpu.make_async_copy(evolved_ref, out_hbm, sem)
     writing.start()
-    mix = mix_ref[...]
+    mix = mixing(gram_ref[...], count)
     factor_ref[...] = full_dot(image_ref[...], mix).astype(BF16)
-    result = full_dot(carried_ref[...], mix) * scale
+    result = full_dot(carried_ref[...], mix) * (count ** -0.5)
     ny = core_ref.shape[2]
     core_ref[0, 0] = result[:ny]
     core_ref[0, 1] = result[ny:]
@@ -499,7 +491,7 @@
     hbm = pl.BlockSpec(memory_space=pltpu.HBM)
     vmem = pl.BlockSpec(memory_space=pltpu.VMEM)
     dma = pltpu.SemaphoreType.DMA
-    evolved, mix, carried, image = pl.pallas_call(
+    evolved, gram, carried, image = pl.pallas_call(
         kernel,
         out_shape=(
             jax.ShapeDtypeStruct(initial_state.shape, F32),
@@ -564,7 +556,7 @@
         ),
     )(*(pltpu.with_memory_space_constraint(x, pltpu.HBM) for x in operands))
     return pl.pallas_call(
-        functools.partial(finish, float(nx * ngx) ** -0.5),
+        functools.partial(finish, float(nx * ngx)),
         out_shape=(
             jax.ShapeDtypeStruct(initial_state.shape, F32),
             jax.ShapeDtypeStruct((nx // ngy, rank), BF16),
@@ -574,7 +566,7 @@
         out_specs=(hbm, vmem, vmem),
         scratch_shapes=[dma],
         compiler_params=pltpu.CompilerParams(vmem_limit_bytes=8 << 20),
-    )(evolved, mix, carried, image)
+    )(evolved, gram, carried, image)
 
 
 def solution(mesh):

time: 69.8 us -> 67.6 us (0.968)
  Pallas kernels: 69 us -> 66.8 us
    pallas_call x1, Pallas kernels: 67.1 us -> 64.2 us  [shards(): pl.pallas_call(kernel, out_shape=(jax.ShapeDtypeStruct(initial_state.shap...]
where the time goes in v4:
time: 67.6 us; the launch traced here: 67.4 us
  Pallas kernels  66.8 us (99%)
    pallas_call x1, Pallas kernels, shards(): pl.pallas_call(kernel, out_shape=(jax.ShapeDtypeStruct(initial_state.shap...  64.2 us
    pallas_call x1, Pallas kernels, shards(): pl.pallas_call(functools.partial(finish, float(nx * ngx)), out_shape=(jax...  2.55 us

profile of v4, /device:TPU:1, one launch (start us, length us, event | category | flops | bytes accessed | tf_op | source)
XLA Modules:
  0.0 67.4 jit_solution(17699637647014631812)
XLA Ops:
  0.6 64.2 %shard_map.76 = (f32[32,2,64,128]{3,2,1,0:T(8,128)S(1)}, f32[128,128]{1,0:T(8,128)S(1)}, f32[128,128]{1,0:T(8,128)S(1)}, f32[32,128]{1,0:T(8,128)S(1)}) custom-call(f32[32,2,64,128]{3,2,1,0:T(8,128)} %init_hbm.1, f32[3,2,64,128]{3,2,1,0:T(8,128)} %vel_hbm.1, f32[32]{0:T(128)} %kappa_hbm.1, f32[32]{0:T(128)} %rate_hbm.1, bf16[4096,128]{1,0:T(8,128)(2,1)} %basis_hbm.1), custom_call_target="tpu_custom_call" | custom-call | tf_op jit(solution)/shard_map/pallas_call | solution.py:494
  64.9 2.6 %shard_map.77 = (f32[32,2,64,128]{3,2,1,0:T(8,128)}, bf16[32,128]{1,0:T(8,128)(2,1)}, f32[1,2,64,128]{3,2,1,0:T(8,128)}) custom-call(f32[32,2,64,128]{3,2,1,0:T(8,128)S(1)} %get-tuple-element.7.evolved_ref, f32[128,128]{1,0:T(8,128)S(1)} %get-tuple-element.8.gram_ref, f32[128,128]{1,0:T(8,128)S(1)} %get-tuple-element.9.carried_ref, ...), custom_call_target="tpu_custom_call" | custom-call | tf_op jit(solution)/shard_map/pallas_call | solution.py:558

commit v5 on v4

--- a/solution.py
+++ b/solution.py
@@ -9,8 +9,10 @@
 
 SECTIONS = 4
 NS_STEPS = 5
-GROUPS = 4
-UNROLL = 2
+EARLY_STEPS = 3
+GROUPS = 8
+PLANES = 4
+UNROLL = 4
 VMEM_LIMIT = 32 << 20
 MESH = pl.DeviceIdType.MESH
 F32 = jnp.float32
@@ -42,25 +44,32 @@
     return terms[0]
 
 
-def mixing(gram, count):
+def identity_like(gram):
     row = lax.broadcasted_iota(jnp.int32, gram.shape, 0)
     column = lax.broadcasted_iota(jnp.int32, gram.shape, 1)
-    identity = jnp.where(row == column, 1.0, 0.0).astype(F32)
+    return jnp.where(row == column, 1.0, 0.0).astype(F32)
+
+
+def scaled(gram, count):
+    identity = identity_like(gram)
     trace = jnp.sum(gram * identity, keepdims=True)
     squared = count / (trace + 1e-6)
-    gram = gram * (squared / count)
-    mix = jnp.sqrt(squared) * identity
-    for step in range(NS_STEPS):
+    return gram * (squared / count), jnp.sqrt(squared) * identity
+
+
+def newton_schulz(gram, mix, steps):
+    identity = identity_like(gram)
+    for step in steps:
         poly = 1.5 * identity - 0.5 * gram
         mix = full_dot(mix, poly)
         if step < NS_STEPS - 1:
             gram = full_dot(poly, full_dot(gram, poly))
-    return mix
+    return gram, mix
 
 
 def kernel(
     init_hbm, vel_hbm, kappa_hbm, rate_hbm, basis_hbm,
-    evolved_ref, gram_ref, carried_ref, image_ref,
+    evolved_ref, gram_ref, mix_ref, carried_ref, image_ref,
     state, state_b, vel, kappa_ref, rate_ref, basis, halos, x_send, x_recv, y_send, y_recv,
     pairs, outbox, pairs_t, part_box, part_sum, carry_box, carry_sum, proj, half_send, half_recv, image_part, image_pair, image_own, gram_part, gram_sum, gram_all,
     load_sem, xs_sem, xr_sem, ys_sem, yr_sem, cs_sem, cr_sem, as_sem, ar_sem, gs_sem, gr_sem, is_sem, ir_sem, hs_sem, hr_sem, ps_sem, pr_sem, ms_sem, mr_sem, ts_sem, tr_sem,
@@ -78,6 +87,8 @@
     sibling = gx + 1 - 2 * core
     own_lanes = pl.ds(pl.multiple_of(core * 128, 128), 128)
     pairs_per = per // 2
+    in_a_plane = species // PLANES
+    line = in_a_plane // 2
     lane = lax.broadcasted_iota(jnp.int32, (ny, 128), 1)
     pair = lane // 2
 
@@ -246,10 +257,8 @@
         if last:
             for box, parity in ((outbox, 1 - core), (pairs, core)):
 
-                @pl.loop(0, per, step=2 * UNROLL)
-                def _(j):
-                    for i in range(UNROLL):
-                        step(j + 2 * i + parity, box)
+                for i in range(pairs_per):
+                    step(2 * i + parity, box)
 
                 if box is outbox:
                     pair_copy(g).start()
@@ -273,26 +282,29 @@
 
     load_basis.wait()
 
-    def group_parts(g):
-        pair_copy(g).wait_recv()
-        make_parts(part_box, g * pairs_per, pairs_per, basis[...])
-
-        @pl.loop(0, pairs_per)
+    def plane_parts(p):
+        for g in range(GROUPS // PLANES):
+            pair_copy(p * (GROUPS // PLANES) + g).wait_recv()
+        make_parts(part_box, p * line, line, basis[...])
+
+        @pl.loop(0, line)
         def _(d):
-            i = g * pairs_per + lax.rem(chip + d, pairs_per)
+            i = p * line + lax.rem(chip + d, line)
 
             @pl.when(i != chip)
             def _():
                 part_copy(part_box, part_sum, 0, i).start()
 
-    @pl.loop(0, GROUPS)
-    def _(g):
-        advance(SECTIONS - 1, g, buffers[(SECTIONS - 1) % 2], None)
-        @pl.when(g > 0)
+    @pl.loop(0, PLANES)
+    def _(p):
+        for g in range(GROUPS // PLANES):
+            advance(SECTIONS - 1, p * (GROUPS // PLANES) + g, buffers[(SECTIONS - 1) % 2], None)
+
+        @pl.when(p > 0)
         def _():
-            group_parts(g - 1)
-
-    group_parts(GROUPS - 1)
+            plane_parts(p - 1)
+
+    plane_parts(PLANES - 1)
 
     @pl.loop(0, half, step=2)
     def _(i):
@@ -302,13 +314,13 @@
     def block(x):
         return pl.ds(pl.multiple_of(x // 2 * 128, 128), 128)
 
-    plane = gx // per
+    plane = gx // in_a_plane
 
     def in_plane(x, d):
-        return x // per * per + lax.rem(x + 2 * d, per)
+        return x // in_a_plane * in_a_plane + lax.rem(x + 2 * d, in_a_plane)
 
     def other_plane(x, d):
-        return lax.rem(x + d * per, ngx)
+        return lax.rem(x + d * in_a_plane, ngx)
 
     def send(x, peer):
         pltpu.make_async_remote_copy(
@@ -332,17 +344,17 @@
     for d in order:
         send(gx, in_plane(gx, d))
 
-    @pl.loop(0, GROUPS)
+    @pl.loop(0, PLANES)
     def _(p):
         @pl.when(p != plane)
         def _():
-            x = p * per + lax.rem(gx, per)
+            x = p * in_a_plane + lax.rem(gx, in_a_plane)
             arrival(x)
             for d in order:
                 send(x, in_plane(gx, d))
 
     for d in order:
-        for f in range(GROUPS):
+        for f in range(PLANES):
             arrival(other_plane(in_plane(gx, d), f))
 
     def image_half(c):
@@ -415,7 +427,7 @@
 
     @pl.loop(1, half)
     def _(d):
-        gram_copy(d).start()
+        gram_copy(lax.rem(5 * d, half)).start()
 
     @pl.loop(0, half, step=8)
     def _(i):
@@ -423,7 +435,7 @@
 
     @pl.loop(1, half)
     def _(d):
-        part_copy(carry_box, carry_sum, 1, lax.rem(chip + d, half)).start()
+        part_copy(carry_box, carry_sum, 1, lax.rem(chip + 5 * d, half)).start()
 
     arrived = all_of(gram_sum, half - 1)
     pltpu.make_async_copy(arrived, arrived, mr_sem).wait()
@@ -446,7 +458,9 @@
     arrived = all_of(gram_all, 16 * len(others))
     pltpu.make_async_copy(arrived, arrived, tr_sem).wait()
 
-    gram_ref[...] = gram_all[...]
+    gram, mix = newton_schulz(*scaled(gram_all[...], 128.0 * ngx), range(EARLY_STEPS))
+    gram_ref[...] = gram
+    mix_ref[...] = mix
     carried_ref[...] = summed(carry_box, carry_sum, 1)
     image_ref[...] = image_own[pl.ds(pl.multiple_of(gy * 32, 32), 32), :]
 
@@ -469,10 +483,10 @@
     pltpu.make_async_copy(sent, sent, is_sem).wait()
 
 
-def finish(count, evolved_ref, gram_ref, carried_ref, image_ref, out_hbm, factor_ref, core_ref, sem):
+def finish(count, evolved_ref, gram_ref, mix_ref, carried_ref, image_ref, out_hbm, factor_ref, core_ref, sem):
     writing = pltpu.make_async_copy(evolved_ref, out_hbm, sem)
     writing.start()
-    mix = mixing(gram_ref[...], count)
+    _, mix = newton_schulz(gram_ref[...], mix_ref[...], range(EARLY_STEPS, NS_STEPS))
     factor_ref[...] = full_dot(image_ref[...], mix).astype(BF16)
     result = full_dot(carried_ref[...], mix) * (count ** -0.5)
     ny = core_ref.shape[2]
@@ -491,16 +505,17 @@
     hbm = pl.BlockSpec(memory_space=pltpu.HBM)
     vmem = pl.BlockSpec(memory_space=pltpu.VMEM)
     dma = pltpu.SemaphoreType.DMA
-    evolved, gram, carried, image = pl.pallas_call(
+    evolved, gram, mix, carried, image = pl.pallas_call(
         kernel,
         out_shape=(
             jax.ShapeDtypeStruct(initial_state.shape, F32),
+            jax.ShapeDtypeStruct((rank, rank), F32),
             jax.ShapeDtypeStruct((rank, rank), F32),
             jax.ShapeDtypeStruct((nz * ny, rank), F32),
             jax.ShapeDtypeStruct((nx // ngy, rank), F32),
         ),
         in_specs=[hbm] * 5,
-        out_specs=(vmem,) * 4,
+        out_specs=(vmem,) * 5,
         scratch_shapes=[
             pltpu.VMEM((species, nz, ny + 16, nx), F32),
             pltpu.VMEM((species, nz, ny + 16, nx), F32),
@@ -562,11 +577,11 @@
             jax.ShapeDtypeStruct((nx // ngy, rank), BF16),
             jax.ShapeDtypeStruct((1, nz, ny, rank), F32),
         ),
-        in_specs=[pl.BlockSpec(memory_space=pl.ANY), vmem, vmem, vmem],
+        in_specs=[pl.BlockSpec(memory_space=pl.ANY), vmem, vmem, vmem, vmem],
         out_specs=(hbm, vmem, vmem),
         scratch_shapes=[dma],
         compiler_params=pltpu.CompilerParams(vmem_limit_bytes=8 << 20),
-    )(evolved, gram, carried, image)
+    )(evolved, gram, mix, carried, image)
 
 
 def solution(mesh):

time: 67.6 us -> 67 us (level)
  no operation moved by 1% of the time
where the time goes in v5:
time: 67 us; the launch traced here: 66.9 us
  Pallas kernels  66.2 us (99%)
    pallas_call x1, Pallas kernels, shards(): pl.pallas_call(kernel, out_shape=(jax.ShapeDtypeStruct(initial_state.shap...  64.3 us
    pallas_call x1, Pallas kernels, shards(): pl.pallas_call(functools.partial(finish, float(nx * ngx)), out_shape=(jax...  1.97 us

profile of v5, /device:TPU:1, one launch (start us, length us, event | category | flops | bytes accessed | tf_op | source)
XLA Modules:
  0.0 66.9 jit_solution(5054563331657899683)
XLA Ops:
  0.6 64.3 %shard_map.76 = (f32[32,2,64,128]{3,2,1,0:T(8,128)S(1)}, f32[128,128]{1,0:T(8,128)S(1)}, f32[128,128]{1,0:T(8,128)S(1)}, f32[128,128]{1,0:T(8,128)S(1)}, f32[32,128]{1,0:T(8,128)S(1)}) custom-call(f32[32,2,64,128]{3,2,1,0:T(8,128)} %init_hbm.1, f32[3,2,64,128]{3,2,1,0:T(8,128)} %vel_hbm.1, f32[32]{0:T(128)} %kappa_hbm.1, f32[32]{0:T(128)} %rate_hbm.1, ...), custom_call_target="tpu_custom_call" | custom-call | tf_op jit(solution)/shard_map/pallas_call | solution.py:508
  64.9 2.0 %shard_map.77 = (f32[32,2,64,128]{3,2,1,0:T(8,128)}, bf16[32,128]{1,0:T(8,128)(2,1)}, f32[1,2,64,128]{3,2,1,0:T(8,128)}) custom-call(f32[32,2,64,128]{3,2,1,0:T(8,128)S(1)} %get-tuple-element.8.evolved_ref, f32[128,128]{1,0:T(8,128)S(1)} %get-tuple-element.9.gram_ref, f32[128,128]{1,0:T(8,128)S(1)} %get-tuple-element.10.mix_ref, ...), custom_call_target="tpu_custom_call" | custom-call | tf_op jit(solution)/shard_map/pallas_call | solution.py:573

commit v6 on v5

--- a/solution.py
+++ b/solution.py
@@ -92,14 +92,21 @@
     lane = lax.broadcasted_iota(jnp.int32, (ny, 128), 1)
     pair = lane // 2
 
-    load_state = pltpu.make_async_copy(init_hbm, state.at[:, :, pl.ds(8, ny), :], load_sem.at[0])
+    def load_state(g):
+        return pltpu.make_async_copy(
+            init_hbm.at[pl.ds(g * per, per)],
+            state.at[pl.ds(g * per, per), :, pl.ds(8, ny), :],
+            load_sem.at[4 + g],
+        )
+
     load_vel = pltpu.make_async_copy(vel_hbm, vel, load_sem.at[1])
     load_kappa = pltpu.make_async_copy(kappa_hbm, kappa_ref, load_sem.at[2])
     load_rate = pltpu.make_async_copy(rate_hbm, rate_ref, load_sem.at[3])
     barrier = pltpu.get_barrier_semaphore()
     for peer in (left, right):
         pl.semaphore_signal(barrier, 1, device_id={"gx": peer}, device_id_type=MESH)
-    load_state.start()
+    for g in range(GROUPS):
+        load_state(g).start()
 
     @pl.loop(1, ngy)
     def _(d):
@@ -186,20 +193,19 @@
         y_copy(e, True).start()
         y_copy(e, False).start()
 
-    load_state.wait()
-
-    @pl.loop(0, GROUPS)
+    load_state(0).wait()
+    pack_edges(0, state, 0)
+    pl.semaphore_wait(barrier, half + 2 * ngy - 1)
+    send_edges(0)
+
+    @pl.loop(1, GROUPS)
     def _(g):
+        load_state(g).wait()
         pack_edges(g, state, g * per)
-
-    pl.semaphore_wait(barrier, half + 2 * ngy - 1)
-
-    @pl.loop(0, GROUPS)
-    def _(g):
         send_edges(g)
 
     basis_rows = pl.ds(pl.multiple_of(chip * 256, 256), 256)
-    load_basis = pltpu.make_async_copy(basis_hbm.at[basis_rows], basis, load_sem.at[4])
+    load_basis = pltpu.make_async_copy(basis_hbm.at[basis_rows], basis, load_sem.at[0])
     load_basis.start()
     load_vel.wait()
     vel[...] = vel[...] * 0.5
@@ -255,13 +261,11 @@
                     new[s, z, pl.ds(8, ny), :] = result
 
         if last:
-            for box, parity in ((outbox, 1 - core), (pairs, core)):
-
-                for i in range(pairs_per):
-                    step(2 * i + parity, box)
-
-                if box is outbox:
-                    pair_copy(g).start()
+            for i in range(pairs_per):
+                step(2 * i + 1 - core, outbox)
+            for i in range(pairs_per):
+                step(2 * i + core, pairs)
+            pair_copy(g).start()
         else:
 
             @pl.loop(0, per, step=UNROLL)
@@ -544,7 +548,7 @@
             pltpu.VMEM((rank, rank), F32),
             pltpu.VMEM((ngx // 2, rank // (2 * ngy), rank), F32),
             pltpu.VMEM((rank, rank), F32),
-            dma((5,)),
+            dma((GROUPS + 4,)),
             dma((2,)),
             dma((exchanges,)),
             dma((2,)),

time: 67 us -> 67 us (level)
  no operation moved by 1% of the time
where the time goes in v6:
time: 67 us; the launch traced here: 66.9 us
  Pallas kernels  66.2 us (99%)
    pallas_call x1, Pallas kernels, shards(): pl.pallas_call(kernel, out_shape=(jax.ShapeDtypeStruct(initial_state.shap...  64.3 us
    pallas_call x1, Pallas kernels, shards(): pl.pallas_call(functools.partial(finish, float(nx * ngx)), out_shape=(jax...  1.97 us

profile of v6, /device:TPU:1, one launch (start us, length us, event | category | flops | bytes accessed | tf_op | source)
XLA Modules:
  0.0 66.9 jit_solution(6628869652022084372)
XLA Ops:
  0.6 64.3 %shard_map.76 = (f32[32,2,64,128]{3,2,1,0:T(8,128)S(1)}, f32[128,128]{1,0:T(8,128)S(1)}, f32[128,128]{1,0:T(8,128)S(1)}, f32[128,128]{1,0:T(8,128)S(1)}, f32[32,128]{1,0:T(8,128)S(1)}) custom-call(f32[32,2,64,128]{3,2,1,0:T(8,128)} %init_hbm.1, f32[3,2,64,128]{3,2,1,0:T(8,128)} %vel_hbm.1, f32[32]{0:T(128)} %kappa_hbm.1, f32[32]{0:T(128)} %rate_hbm.1, ...), custom_call_target="tpu_custom_call" | custom-call | tf_op jit(solution)/shard_map/pallas_call | solution.py:512
  64.9 2.0 %shard_map.77 = (f32[32,2,64,128]{3,2,1,0:T(8,128)}, bf16[32,128]{1,0:T(8,128)(2,1)}, f32[1,2,64,128]{3,2,1,0:T(8,128)}) custom-call(f32[32,2,64,128]{3,2,1,0:T(8,128)S(1)} %get-tuple-element.8.evolved_ref, f32[128,128]{1,0:T(8,128)S(1)} %get-tuple-element.9.gram_ref, f32[128,128]{1,0:T(8,128)S(1)} %get-tuple-element.10.mix_ref, ...), custom_call_target="tpu_custom_call" | custom-call | tf_op jit(solution)/shard_map/pallas_call | solution.py:577

commit v7 on v6

--- a/solution.py
+++ b/solution.py
@@ -72,7 +72,7 @@
     evolved_ref, gram_ref, mix_ref, carried_ref, image_ref,
     state, state_b, vel, kappa_ref, rate_ref, basis, halos, x_send, x_recv, y_send, y_recv,
     pairs, outbox, pairs_t, part_box, part_sum, carry_box, carry_sum, proj, half_send, half_recv, image_part, image_pair, image_own, gram_part, gram_sum, gram_all,
-    load_sem, xs_sem, xr_sem, ys_sem, yr_sem, cs_sem, cr_sem, as_sem, ar_sem, gs_sem, gr_sem, is_sem, ir_sem, hs_sem, hr_sem, ps_sem, pr_sem, ms_sem, mr_sem, ts_sem, tr_sem,
+    load_sem, xs_sem, xr_sem, ys_sem, cs_sem, cr_sem, as_sem, ar_sem, gs_sem, gr_sem, is_sem, ir_sem, hs_sem, hr_sem, ps_sem, pr_sem, ms_sem, mr_sem, ts_sem, tr_sem,
 ):
     species = state.shape[0]
     ny = state.shape[2] - 16
@@ -139,7 +139,7 @@
             src_ref=y_send.at[d, e],
             dst_ref=y_recv.at[e, d],
             send_sem=ys_sem.at[d],
-            recv_sem=yr_sem.at[e],
+            recv_sem=xr_sem.at[e],
             device_id={"gy": south if to_south else north},
             device_id_type=MESH,
         )
@@ -213,11 +213,12 @@
     load_kappa.wait()
     load_rate.wait()
 
+    assert 2 * ny * 128 * 2 + 2 * 2 * per * 128 * 4 == (ny + 16) * 128 * 4
+
     def advance(k, g, now, new):
         e = k * GROUPS + g
         last = k == SECTIONS - 1
-        pltpu.make_async_copy(x_recv.at[e], x_recv.at[e], xr_sem.at[e]).wait()
-        pltpu.make_async_copy(y_recv.at[e], y_recv.at[e], yr_sem.at[e]).wait()
+        pltpu.make_async_copy(state.at[0, 0], state.at[0, 0], xr_sem.at[e]).wait()
 
         wide = lax.broadcasted_iota(jnp.int32, halos.shape, 1)
         halos[...] = jnp.where(
@@ -326,27 +327,27 @@
     def other_plane(x, d):
         return lax.rem(x + d * in_a_plane, ngx)
 
-    def send(x, peer):
+    def send(x, peer, arrives):
         pltpu.make_async_remote_copy(
             src_ref=proj.at[block(x)],
             dst_ref=proj.at[block(x)],
             send_sem=gs_sem,
-            recv_sem=gr_sem.at[x // 2],
+            recv_sem=gr_sem.at[arrives],
             device_id={"gx": peer},
             device_id_type=MESH,
         ).start()
 
     def arrival(x):
-        pltpu.make_async_copy(proj.at[block(x)], proj.at[block(x)], gr_sem.at[x // 2]).wait()
+        pltpu.make_async_copy(proj.at[block(x)], proj.at[block(x)], gr_sem.at[x // in_a_plane]).wait()
 
     order = (1, 3, 2)
 
     proj[block(gx), :] = summed(part_box, part_sum, 0).astype(BF16)
 
     for d in order:
-        send(gx, other_plane(gx, d))
+        send(gx, other_plane(gx, d), plane)
     for d in order:
-        send(gx, in_plane(gx, d))
+        send(gx, in_plane(gx, d), PLANES)
 
     @pl.loop(0, PLANES)
     def _(p):
@@ -355,11 +356,10 @@
             x = p * in_a_plane + lax.rem(gx, in_a_plane)
             arrival(x)
             for d in order:
-                send(x, in_plane(gx, d))
-
-    for d in order:
-        for f in range(PLANES):
-            arrival(other_plane(in_plane(gx, d), f))
+                send(x, in_plane(gx, d), PLANES)
+
+    arrived = all_of(proj, (half - PLANES) * 128)
+    pltpu.make_async_copy(arrived, arrived, gr_sem.at[PLANES]).wait()
 
     def image_half(c):
         rows = pl.ds(pl.multiple_of(c * 128, 128), 128)
@@ -552,13 +552,12 @@
             dma((2,)),
             dma((exchanges,)),
             dma((2,)),
-            dma((exchanges,)),
             dma,
             dma((GROUPS,)),
             dma((2,)),
             dma((2,)),
             dma,
-            dma((ngx // 2,)),
+            dma((PLANES + 1,)),
             dma,
             dma,
             dma,

time: 67 us -> 66.6 us (level)
  no operation moved by 1% of the time
where the time goes in v7:
time: 66.6 us; the launch traced here: 66.5 us
  Pallas kernels  65.8 us (99%)
    pallas_call x1, Pallas kernels, shards(): pl.pallas_call(kernel, out_shape=(jax.ShapeDtypeStruct(initial_state.shap...  63.8 us
    pallas_call x1, Pallas kernels, shards(): pl.pallas_call(functools.partial(finish, float(nx * ngx)), out_shape=(jax...  1.97 us

profile of v7, /device:TPU:1, one launch (start us, length us, event | category | flops | bytes accessed | tf_op | source)
XLA Modules:
  0.0 66.5 jit_solution(15444353144827102188)
XLA Ops:
  0.6 63.8 %shard_map.76 = (f32[32,2,64,128]{3,2,1,0:T(8,128)S(1)}, f32[128,128]{1,0:T(8,128)S(1)}, f32[128,128]{1,0:T(8,128)S(1)}, f32[128,128]{1,0:T(8,128)S(1)}, f32[32,128]{1,0:T(8,128)S(1)}) custom-call(f32[32,2,64,128]{3,2,1,0:T(8,128)} %init_hbm.1, f32[3,2,64,128]{3,2,1,0:T(8,128)} %vel_hbm.1, f32[32]{0:T(128)} %kappa_hbm.1, f32[32]{0:T(128)} %rate_hbm.1, ...), custom_call_target="tpu_custom_call" | custom-call | tf_op jit(solution)/shard_map/pallas_call | solution.py:512
  64.5 2.0 %shard_map.77 = (f32[32,2,64,128]{3,2,1,0:T(8,128)}, bf16[32,128]{1,0:T(8,128)(2,1)}, f32[1,2,64,128]{3,2,1,0:T(8,128)}) custom-call(f32[32,2,64,128]{3,2,1,0:T(8,128)S(1)} %get-tuple-element.8.evolved_ref, f32[128,128]{1,0:T(8,128)S(1)} %get-tuple-element.9.gram_ref, f32[128,128]{1,0:T(8,128)S(1)} %get-tuple-element.10.mix_ref, ...), custom_call_target="tpu_custom_call" | custom-call | tf_op jit(solution)/shard_map/pallas_call | solution.py:576

commit v8 on v7

--- a/solution.py
+++ b/solution.py
@@ -9,7 +9,7 @@
 
 SECTIONS = 4
 NS_STEPS = 5
-EARLY_STEPS = 3
+EARLY_STEPS = 2
 GROUPS = 8
 PLANES = 4
 UNROLL = 4

time: 66.6 us -> 66.6 us (level)
  no operation moved by 1% of the time
where the time goes in v8:
time: 66.6 us; the launch traced here: 66.4 us
  Pallas kernels  65.8 us (99%)
    pallas_call x1, Pallas kernels, shards(): pl.pallas_call(kernel, out_shape=(jax.ShapeDtypeStruct(initial_state.shap...  63.8 us
    pallas_call x1, Pallas kernels, shards(): pl.pallas_call(functools.partial(finish, float(nx * ngx)), out_shape=(jax...  1.97 us

profile of v8, /device:TPU:1, one launch (start us, length us, event | category | flops | bytes accessed | tf_op | source)
XLA Modules:
  0.0 66.4 jit_solution(854284673460009770)
XLA Ops:
  0.6 63.8 %shard_map.76 = (f32[32,2,64,128]{3,2,1,0:T(8,128)S(1)}, f32[128,128]{1,0:T(8,128)S(1)}, f32[128,128]{1,0:T(8,128)S(1)}, f32[128,128]{1,0:T(8,128)S(1)}, f32[32,128]{1,0:T(8,128)S(1)}) custom-call(f32[32,2,64,128]{3,2,1,0:T(8,128)} %init_hbm.1, f32[3,2,64,128]{3,2,1,0:T(8,128)} %vel_hbm.1, f32[32]{0:T(128)} %kappa_hbm.1, f32[32]{0:T(128)} %rate_hbm.1, ...), custom_call_target="tpu_custom_call" | custom-call | tf_op jit(solution)/shard_map/pallas_call | solution.py:512
  64.5 2.0 %shard_map.77 = (f32[32,2,64,128]{3,2,1,0:T(8,128)}, bf16[32,128]{1,0:T(8,128)(2,1)}, f32[1,2,64,128]{3,2,1,0:T(8,128)}) custom-call(f32[32,2,64,128]{3,2,1,0:T(8,128)S(1)} %get-tuple-element.8.evolved_ref, f32[128,128]{1,0:T(8,128)S(1)} %get-tuple-element.9.gram_ref, f32[128,128]{1,0:T(8,128)S(1)} %get-tuple-element.10.mix_ref, ...), custom_call_target="tpu_custom_call" | custom-call | tf_op jit(solution)/shard_map/pallas_call | solution.py:576
